TPU v7x, 128 devices: a whole 4x4x4 slice. The times are simulated.
128 devices in a mesh: ctx: 32 (over x, y, core), head: 4 (over z).
Axes of the slice: x: 4, y: 4, z: 4, core: 2. Of those that a mesh axis runs over, the one named last changes fastest.
Arguments:
- queries: bfloat16 [2, 8192, 16384], P(None, 'ctx', 'head'), may hold values from -900 to 900
- key_input: bfloat16 [2, 8192, 1024], P(None, 'ctx', 'head'), may hold values from -900 to 900
- values: bfloat16 [2, 8192, 1024], P(None, 'ctx', 'head'), may hold values from -40 to 40
- query_map: bfloat16 [128, 128, 128], P('head'), may hold values from -0.5 to 0.5
- key_map: bfloat16 [8, 128, 128], P('head'), may hold values from -0.5 to 0.5
- out_gain: bfloat16 [16384], P('head'), may hold values from 0.099609375 to 1.8984375
- rank_in: bfloat16 [16384, 512], P('head'), may hold values from -0.046875 to 0.046875
- rank_out: bfloat16 [512, 16384], P(None, 'head'), may hold values from -0.25 to 0.25
Outputs:
- layer_out: bfloat16 [2, 8192, 16384], P(None, 'ctx', 'head')
All inputs are finite; a program needn't handle non-finite values.
Results may differ from a plain program's by a relative error of at most 0.006.
Values may be sent and summed in bfloat16 or wider, within the bound.
A program may use at most 128 MiB of HBM per device.

v0:
```python
import jax
import jax.numpy as jnp
from jax import lax
from jax.sharding import PartitionSpec as P

H = 128
KVH = 8
HD = 128
FEAT = 128


def feature_pair(inputs, weight, form):
    scores = jnp.einsum(form, inputs, weight, preferred_element_type=jnp.float32)
    joined = jnp.concatenate(
        [jax.nn.softmax(scores, axis=-1), jax.nn.softmax(-scores, axis=-1)], axis=-1
    )
    return joined.astype(jnp.bfloat16)


def shards(queries, key_input, values, query_map, key_map, out_gain, rank_in, rank_out):
    seqs_here = queries.shape[0]
    block_len = queries.shape[1]
    kv_local = key_map.shape[0]
    groups = H // KVH
    query_view = queries.reshape(seqs_here, block_len, kv_local, groups, HD)
    key_view = key_input.reshape(seqs_here, block_len, kv_local, HD)
    value_view = values.reshape(seqs_here, block_len, kv_local, HD)
    qmap_view = query_map.reshape(kv_local, groups, HD, FEAT)
    feat_key = feature_pair(key_view, key_map, "sbgd,gdf->sbgf")
    states = jnp.einsum("sbgf,sbgd->sgfd", feat_key, value_view, preferred_element_type=jnp.float32)
    key_sums = jnp.sum(feat_key.astype(jnp.float32), axis=1)
    my_index = lax.axis_index("ctx")
    pieces = (
        lax.all_gather(states[None], "ctx", axis=0, tiled=True),
        lax.all_gather(key_sums[None], "ctx", axis=0, tiled=True),
    )
    lower = jnp.arange(pieces[0].shape[0], dtype=jnp.int32) < my_index
    state_part = jnp.sum(jnp.where(lower[:, None, None, None, None], pieces[0], 0.0), axis=0)
    sum_part = jnp.sum(jnp.where(lower[:, None, None, None], pieces[1], 0.0), axis=0)
    feat_query = feature_pair(query_view, qmap_view, "sbgqd,gqdf->sbgqf")
    carried_num = jnp.einsum(
        "sbgqf,sgfd->sbgqd",
        feat_query,
        state_part.astype(jnp.bfloat16),
        preferred_element_type=jnp.float32,
    )
    carried_den = jnp.einsum(
        "sbgqf,sgf->sbgq",
        feat_query,
        sum_part.astype(jnp.bfloat16),
        preferred_element_type=jnp.float32,
    )
    scores = jnp.einsum(
        "sbgqf,scgf->sgqbc", feat_query, feat_key, preferred_element_type=jnp.float32
    )
    causal = jnp.arange(block_len)[:, None] >= jnp.arange(block_len)[None, :]
    scores = jnp.where(causal, scores, 0.0)
    local_den = jnp.transpose(jnp.sum(scores, axis=-1), (0, 3, 1, 2))
    local_num = jnp.einsum(
        "sgqbc,scgd->sbgqd",
        scores.astype(jnp.bfloat16),
        value_view,
        preferred_element_type=jnp.float32,
    )
    attended = (local_num + carried_num) / (local_den + carried_den)[..., None]
    attended = attended.reshape(seqs_here * block_len, kv_local * groups * HD)
    square_sum = lax.psum(jnp.sum(attended * attended, axis=-1), "head")
    factor = lax.rsqrt(square_sum / (H * HD) + 1e-05)
    normed = (attended * factor[:, None] * out_gain.astype(jnp.float32)).astype(jnp.bfloat16)
    partial_rank = jnp.dot(normed, rank_in, preferred_element_type=jnp.float32)
    reduced = lax.psum(partial_rank, "head").astype(jnp.bfloat16)
    result = jnp.dot(reduced, rank_out, preferred_element_type=jnp.float32).astype(jnp.bfloat16)
    return result.reshape(seqs_here, block_len, rank_out.shape[1])


def solution(mesh):
    in_specs = (
        P(None, "ctx", "head"),
        P(None, "ctx", "head"),
        P(None, "ctx", "head"),
        P("head", None, None),
        P("head", None, None),
        P("head"),
        P("head", None),
        P(None, "head"),
    )
    out_specs = P(None, "ctx", "head")
    return jax.shard_map(shards, mesh=mesh, in_specs=in_specs, out_specs=out_specs, check_vma=False)
```

profile of v0, /device:TPU:0, one launch (start us, length us, event | category | flops | bytes accessed | tf_op | source)
XLA Modules:
  0.0 189.5 jit_solution(14557753929164909112)
XLA Ops:
  6.5 0.0 all-gather.4.cloned.1.call-start
  6.5 1.4 fusion.63
  8.0 1.3 fusion.68
  9.3 0.1 divide_convert_fusion.2
  9.4 0.1 pad_maximum_fusion.1
  9.5 2.1 %fusion.34 = f32[2,2,256,128]{3,2,1,0:T(8,128)} fusion(bf16[2,256,2,256]{1,3,0,2:T(8,128)(2,1)S(1)} %get-tuple-element.5, bf16[2,256,256]{2,1,0:T(8,128)(2,1)} %param.10), kind=kOutput, calls=%fused_computation.45 | convolution fusion | flops 67108864 | bytes 1310720 | tf_op jit(solution)/shard_map/sbgf,sbgd->sgfd/dot_general | solution.py:30
  11.6 0.0 all-gather.4.cloned.1.call-update
  11.6 1.0 reshape.41
  12.6 0.7 convert_element_type.30
  13.3 0.2 convert_reduce_fusion
  13.6 3.4 %copy.71 = bf16[64,8,32,128]{3,2,1,0:T(8,128)(2,1)S(1)} copy(bf16[64,8,32,128]{3,1,2,0:T(8,128)(2,1)} %bitcast.132) | data formatting | bytes 8388608
  17.0 25.3 %all-gather.1 = f32[64,2,256]{2,1,0:T(2,128)S(1)} all-gather(f32[2,2,256]{2,1,0:T(2,128)S(1)} %copy.44), channel_id=3, replica_groups=mesh['ctx'=32,'head'=4] {'ctx'}, dimensions={0}, use_global_device_ids=true | all-gather | bytes 135168 | tf_op jit(solution)/shard_map/all_gather | solution.py:35
  42.3 0.1 select_reduce_fusion.1
  42.4 4.8 %fusion.23 = f32[2,16,128,2,256]{4,2,3,1,0:T(8,128)S(1)} fusion(bf16[2,16,128,128,1]{3,2,4,1,0:T(8,128)(2,1)S(1)} %bitcast.129, bf16[2,256,2,16,128]{4,3,2,1,0:T(8,128)(2,1)S(1)} %bitcast.131), kind=kOutput, calls=%fused_computation.33 | convolution fusion | flops 536870912 | bytes 13631488 | tf_op jit(solution)/shard_map/sbgqd,gqdf->sbgqf/dot_general | solution.py:13
  47.2 9.3 %fusion.61 = (f32[2,256,2,16]{1,0,3,2:T(2,128)S(1)}, f32[2,256,2,16,128]{1,4,0,3,2:T(8,128)S(1)}) fusion(f32[2,16,128,2,256]{4,2,3,1,0:T(8,128)S(1)} %fusion.23), kind=kOutput, calls=%fused_computation.69 | output fusion | flops 8388735 | bytes 16842752 | tf_op jit(solution)/shard_map/sub | solution.py:15
  56.6 4.7 %fusion.62 = (f32[2,256,2,16]{1,0,3,2:T(2,128)S(1)}, f32[2,256,2,16,128]{1,4,0,3,2:T(8,128)}) fusion(f32[2,16,128,2,256]{4,2,3,1,0:T(8,128)S(1)} %fusion.23), kind=kOutput, calls=%fused_computation.70 | output fusion | flops 4194431 | bytes 16842752 | tf_op jit(solution)/shard_map/sub | solution.py:15
  61.3 5.1 %divide_convert_fusion = (bf16[2,256,2,16,128]{1,4,0,3,2:T(8,128)(2,1)S(1)}, bf16[2,256,2,16,128]{1,4,0,3,2:T(8,128)(2,1)S(1)}) fusion(f32[2,256,2,16,128]{1,4,0,3,2:T(8,128)S(1)} %get-tuple-element.8, f32[2,256,2,16]{1,0,3,2:T(2,128)S(1)} %get-tuple-element.7, f32[2,256,2,16,128]{1,4,0,3,2:T(8,128)} %get-tuple-element.10, ...), kind=kLoop, calls=%fused_computation.20 | loop fusion | flops 8388608 | bytes 25296896 | tf_op jit(solution)/shard_map/convert.1
  66.3 0.0 copy-start.2
  66.4 2.0 %copy-done.2 = bf16[2,256,2,16,128]{1,4,0,3,2:T(8,128)(2,1)} copy-done((bf16[2,256,2,16,128]{1,4,0,3,2:T(8,128)(2,1)}, bf16[2,256,2,16,128]{1,4,0,3,2:T(8,128)(2,1)S(1)}, u32[]{:S(2)}) %copy-start.2) | copy-done | bytes 4194328
  68.4 1.3 copy-done.3
  69.7 5.5 %fusion.14 = f32[2,2,1,256,16]{2,3,4,1,0:T(8,128)} fusion(bf16[2,2,256,1,1]{2,1,0,3,4:T(2,128)(2,1)S(1)} %bitcast.136, bf16[2,256,2,16,128]{1,4,0,3,2:T(8,128)(2,1)S(1)} %get-tuple-element.19, bf16[2,256,2,16,128]{1,4,0,3,2:T(8,128)(2,1)S(1)} %get-tuple-element.20), kind=kOutput, calls=%fused_computation.25 | convolution fusion | flops 25165824 | bytes 8456192 | tf_op jit(solution)/shard_map/sbgqf,sgf->sbgq/dot_general | solution.py:47
  75.2 5.2 %copy.56 = f32[2,2,1,256,16]{3,4,1,0,2:T(8,128)S(1)} copy(f32[2,2,1,256,16]{2,3,4,1,0:T(8,128)} %fusion.14) | data formatting | bytes 131072 | tf_op jit(solution)/shard_map/sbgqf,sgf->sbgq/dot_general | solution.py:47
  80.5 5.0 %fusion.4 = (f32[2,2,16,256]{3,2,1,0:T(8,128)S(1)}, bf16[2,2,256,256,16]{3,2,4,1,0:T(8,128)(2,1)S(1)}) fusion(pred[256,256]{0,1:T(8,128)(4,1)S(1)} %iota_compare_fusion, bf16[2,256,2,256,1]{1,3,0,2,4:T(8,128)(2,1)S(1)} %get-tuple-element.6, bf16[2,256,2,16,128]{1,4,0,3,2:T(8,128)(2,1)} %copy-done.2, bf16[2,256,2,16,128]{1,4,0,3,2:T(8,128)(2,1)} %copy-done.3), kind=kOutput, calls=%fused_computation.6 | convolution fusion | flops 2176827392 | bytes 17432576 | tf_op jit(solution)/shard_map/sbgqf,scgf->sgqbc/dot_general | solution.py:53
  85.5 4.6 %fusion.6 = f32[2,2,16,256,128]{3,4,2,1,0:T(8,128)} fusion(bf16[2,2,256,256,16]{3,2,4,1,0:T(8,128)(2,1)S(1)} %get-tuple-element.16, pred[256,256]{0,1:T(8,128)(4,1)S(1)} %iota_compare_fusion, bf16[2,256,2,128,1]{3,2,1,0,4:T(2,128)(2,1)S(1)} %bitcast.133), kind=kOutput, calls=%fused_computation.8 | convolution fusion | flops 1077936128 | bytes 17104896 | tf_op jit(solution)/shard_map/sgqbc,scgd->sbgqd/dot_general | solution.py:59
  90.1 7.5 %select_reduce_fusion = bf16[2,2,256,128]{3,2,1,0:T(8,128)(2,1)S(1)} fusion(f32[32,2,2,256,128]{4,3,2,1,0:T(8,128)} %bitcast.130, pred[32]{0:T(512)(128)(4,1)S(1)} %iota_compare_fusion.1), kind=kLoop, calls=%fused_computation.5 | loop fusion | flops 8257536 | bytes 17039392 | tf_op jit(solution)/shard_map/reduce_sum | solution.py:38
  97.6 9.8 %multiply_reduce_fusion = (f32[2,256]{1,0:T(2,128)S(1)}, f32[2,256,2,16,128]{1,4,3,2,0:T(8,128)}) fusion(f32[2,256,2,16]{1,3,2,0:T(8,128)S(1)} %bitcast_add_fusion.1, bf16[2,2,256,128]{3,2,1,0:T(8,128)(2,1)S(1)} %select_reduce_fusion, f32[2,2,16,256,128]{3,4,2,1,0:T(8,128)} %fusion.6, bf16[2,256,2,16,128]{1,4,0,3,2:T(8,128)(2,1)} %copy-done.2, ...), kind=kOutput, calls=%fused_computation.18 | convolution fusion | flops 1098907136 | bytes 25495552 | tf_op jit(solution)/shard_map/sbgqf,sgfd->sbgqd/dot_general | solution.py:41
  107.4 12.1 %psum.14 = f32[512]{0:T(512)S(1)} all-reduce(f32[512]{0:T(512)S(1)} %bitcast.135), channel_id=1, replica_groups=mesh['ctx'=32,'head'=4] {'head'}, use_global_device_ids=true, to_apply=%region_13.14 | all-reduce | flops 512 | bytes 4096 | tf_op jit(solution)/shard_map/psum | solution.py:67
  119.6 10.3 %copy.45 = f32[2,256,2,16,128]{4,3,2,1,0:T(8,128)} copy(f32[2,256,2,16,128]{1,4,3,2,0:T(8,128)} %get-tuple-element.18) | data formatting | bytes 16777216 | tf_op jit(solution)/shard_map/div | solution.py:65
  129.9 9.4 %reshape.42 = f32[512,4096]{1,0:T(8,128)} reshape(f32[2,256,2,16,128]{4,3,2,1,0:T(8,128)} %copy.45) | data formatting | bytes 16777216 | tf_op jit(solution)/shard_map/reshape | solution.py:66
  139.3 7.0 %fusion.22 = f32[512,512]{1,0:T(8,128)S(1)} fusion(bf16[4096,512]{1,0:T(8,128)(2,1)} %param.14, f32[512,4096]{1,0:T(8,128)} %reshape.42, f32[4096]{0:T(1024)S(1)} %convert_element_type.30, f32[512]{0:T(512)S(1)} %add_rsqrt_fusion), kind=kOutput, calls=%fused_computation.32 | convolution fusion | flops 2153775104 | bytes 13649920 | tf_op jit(solution)/shard_map/dot_general | solution.py:70
  146.3 29.8 %all-reduce.1 = bf16[512,512]{1,0:T(8,128)(2,1)S(1)} all-reduce(f32[512,512]{1,0:T(8,128)S(1)} %fusion.22), channel_id=1, replica_groups=mesh['ctx'=32,'head'=4] {'head'}, use_global_device_ids=true, to_apply=%region_14.15 | all-reduce | flops 262144 | bytes 1572864 | tf_op jit(solution)/shard_map/psum | solution.py:71
  176.1 6.6 %convolution_convert_fusion = bf16[512,4096]{1,0:T(8,128)(2,1)} fusion(bf16[512,4096]{1,0:T(8,128)(2,1)} %param.15, bf16[512,512]{1,0:T(8,128)(2,1)S(1)} %all-reduce.1), kind=kOutput, calls=%fused_computation.31 | convolution fusion | flops 2149580800 | bytes 8912896 | tf_op jit(solution)/shard_map/dot_general | solution.py:72
  (12 shorter events, 0.1 us)
Async XLA Ops:
  6.5 35.9 %copy-start = (bf16[32,128,128]{2,1,0:T(8,128)(2,1)S(1)}, bf16[32,128,128]{2,1,0:T(8,128)(2,1)}, u32[]{:S(2)}) copy-start(bf16[32,128,128]{2,1,0:T(8,128)(2,1)} %param.11) | copy-start | bytes 3145732
  6.5 83.5 %all-gather.4.cloned.1.call-start = ((), (), s32[]{:S(2)}) async-start(), calls=%async_computation | async-start | bytes 17301504 | tf_op jit(solution)/shard_map/all_gather | solution.py:34
  66.3 2.0 %copy-start.2 = (bf16[2,256,2,16,128]{1,4,0,3,2:T(8,128)(2,1)}, bf16[2,256,2,16,128]{1,4,0,3,2:T(8,128)(2,1)S(1)}, u32[]{:S(2)}) copy-start(bf16[2,256,2,16,128]{1,4,0,3,2:T(8,128)(2,1)S(1)} %get-tuple-element.19) | copy-start | bytes 12582916
  66.4 3.3 %copy-start.3 = (bf16[2,256,2,16,128]{1,4,0,3,2:T(8,128)(2,1)}, bf16[2,256,2,16,128]{1,4,0,3,2:T(8,128)(2,1)S(1)}, u32[]{:S(2)}) copy-start(bf16[2,256,2,16,128]{1,4,0,3,2:T(8,128)(2,1)S(1)} %get-tuple-element.20) | copy-start | bytes 12582916
  139.3 43.4 %copy-start.1 = (bf16[32,128,128]{2,1,0:T(8,128)(2,1)S(1)}, bf16[32,128,128]{2,1,0:T(8,128)(2,1)}, u32[]{:S(2)}) copy-start(bf16[32,128,128]{2,1,0:T(8,128)(2,1)} %param.11) | copy-start | bytes 3145732
Sparse Core Ops, SparseCore 0:
  11.7 74.9 all-gather.3
where the time goes:
time: 190 us; the launch traced here: 189 us
  blocking collectives  67.2 us (35%)
  matrix products  48.2 us (25%)
  local copies, waits for them, and re-layouts  32.7 us (17%)
  other arithmetic  27.9 us (15%)
  between operations  13.5 us (7%)
    psum x1, blocking collectives, shards(): reduced = lax.psum(partial_rank, 'head').astype(jnp.bfloat16)  29.8 us
    all_gather x1, blocking collectives, shards(): lax.all_gather(key_sums[None], 'ctx', axis=0, tiled=True)  25.3 us
    psum x1, blocking collectives, shards(): square_sum = lax.psum(jnp.sum(attended * attended, axis=-1), 'head')  12.1 us
    div x1, local copies, waits for them, and re-layouts, shards(): attended = (local_num + carried_num) / (local_den + carried_den)[..., None]  10.3 us
    dot_general x1, matrix products, shards(): jnp.einsum('sbgqf,sgfd->sbgqd', feat_query, state_part.astype(jnp.bfloat1...  9.85 us
    reshape x1, local copies, waits for them, and re-layouts, shards(): attended = attended.reshape(seqs_here * block_len, kv_local * groups * HD)  9.39 us
    sub x1, other arithmetic, feature_pair(): jax.nn.softmax(-scores, axis=-1)  9.3 us
    reduce_sum x1, other arithmetic, shards(): jnp.sum(jnp.where(lower[:, None, None, None, None], pieces[0], 0.0), axis=0)  7.49 us
  transfers between devices with their start and end apart: 1, of which 0 were waited for; matrix products, arithmetic and copies ran while one was open for 26% of the time, Pallas kernels for 0%

commit v1 on v0

v1 whole, which is shorter than its diff:
```python
import functools

import jax
import jax.numpy as jnp
from jax import lax
from jax.experimental import pallas as pl
from jax.experimental.pallas import tpu as pltpu
from jax.sharding import PartitionSpec as P

HD = 128
BLK = 256
SEQS = 2
LOG2E = 1.4426950408889634
MESH = pl.DeviceIdType.MESH
bf16, f32 = jnp.bfloat16, jnp.float32


def nn(a, b):
    return jnp.dot(a, b, preferred_element_type=f32)


def tt(a, b):
    return lax.dot_general(a, b, (((0,), (1,)), ((), ())), preferred_element_type=f32)


def exps(scores):
    scaled = scores * LOG2E
    pos = jnp.exp2(scaled - jnp.max(scaled, axis=0, keepdims=True))
    neg = jnp.exp2(jnp.min(scaled, axis=0, keepdims=True) - scaled)
    return pos, neg, jnp.sum(pos, axis=0, keepdims=True), jnp.sum(neg, axis=0, keepdims=True)


def kernel(nc, nz, feats, q_hbm, k_hbm, v_hbm, qm_hbm, km_hbm, gain_ref, ri_hbm, out_ref,
           q_v, k_v, v_v, qm_v, km_v, ri_v, rit, gcol, fk, vta, pta, fq, wb, att, ssq, part,
           send_e, recv_e, send_p, recv_p, msg, got, red,
           in_sem, s1, r1, s2, r2, s3, r3, s4, r4):
    hl, kvl = qm_v.shape[0], km_v.shape[0]
    groups = hl // kvl
    rank = ri_v.shape[1]
    rb = rank // nz
    rows = send_e.shape[1]
    per = HD // rows
    mc, mz = lax.axis_index("ctx"), lax.axis_index("head")

    loads = [(k_hbm, k_v), (v_hbm, v_v), (km_hbm, km_v), (qm_hbm, qm_v),
             (q_hbm.at[0], q_v.at[0]), (ri_hbm, ri_v), (q_hbm.at[1], q_v.at[1])]
    loads = [pltpu.make_async_copy(a, b, in_sem.at[i]) for i, (a, b) in enumerate(loads)]
    for load in loads:
        load.start()

    barrier = pltpu.get_barrier_semaphore()

    def greet_ctx(i, _):
        pl.semaphore_signal(barrier, inc=1, device_id=(lax.rem(mc + i, nc), mz), device_id_type=MESH)
        return 0

    lax.fori_loop(1, nc, greet_ctx, 0)
    for i in range(1, nz):
        pl.semaphore_signal(barrier, inc=1, device_id=(mc, lax.rem(mz + i, nz)), device_id_type=MESH)

    for load in loads[:3]:
        load.wait()
    first = lax.broadcasted_iota(jnp.int32, (rows, HD), 0) == 0
    for s in range(SEQS):
        for g in range(kvl):
            i = s * kvl + g
            lanes = slice(g * HD, (g + 1) * HD)
            pos, neg, zp, zn = exps(tt(km_v[g], k_v[s, :, lanes]))
            feat = jnp.concatenate([pos * (1.0 / zp), neg * (1.0 / zn)], axis=0).astype(bf16)
            fk[i] = feat.T
            vta[i, 0:HD, :] = v_v[s, :, lanes].T
            vta[i, HD:HD + 16, :] = jnp.ones((16, BLK), bf16)
            state = nn(vta[i], fk[i])
            for p in range(per):
                j = i * per + p
                send_e[j, :, 0:2 * HD] = state[p * rows:(p + 1) * rows].astype(bf16)
                send_e[j, :, 2 * HD:] = jnp.where(
                    first, state[HD:HD + 1, 0:HD], state[HD:HD + 1, HD:2 * HD]).astype(bf16)

    pl.semaphore_wait(barrier, nc - 1 + nz - 1)

    def exchange(src, dst, ssem, rsem, i):
        to = lax.rem(mc + i, nc)
        return pltpu.make_async_remote_copy(
            src_ref=src.at[to], dst_ref=dst.at[mc], send_sem=ssem.at[i], recv_sem=rsem.at[i],
            device_id=(to, mz), device_id_type=MESH)

    def arrival(src, dst, ssem, rsem, i):
        at = lax.rem(mc + nc - i, nc)
        return pltpu.make_async_remote_copy(
            src_ref=src.at[at], dst_ref=dst.at[at], send_sem=ssem.at[i], recv_sem=rsem.at[i],
            device_id=(at, mz), device_id_type=MESH)

    def start1(i, _):
        exchange(send_e, recv_e, s1, r1, i).start()
        return 0

    lax.fori_loop(1, nc, start1, 0)
    recv_e[mc] = send_e[mc]

    for load in loads[3:6]:
        load.wait()

    upper = (lax.broadcasted_iota(jnp.int32, (BLK, BLK), 0)
             <= lax.broadcasted_iota(jnp.int32, (BLK, BLK), 1))

    def features(s, h):
        g = s * kvl + h // groups
        pos, neg, zp, zn = exps(tt(qm_v[h], q_v[s, :, pl.ds(pl.multiple_of(h * HD, HD), HD)]))
        feat = jnp.concatenate([pos, neg * (zp / zn)], axis=0).astype(bf16)
        fq[s * hl + h] = feat
        wb[s * hl + h] = jnp.where(upper, nn(fk[g], feat), 0.0).astype(bf16)

    def prepare(h):
        gain = gain_ref[0:1, pl.ds(pl.multiple_of(h * HD, HD), HD)].astype(f32)
        gcol[h] = jnp.broadcast_to(gain, (HD, HD)).T
        rit[:, pl.ds(pl.multiple_of(h * HD, HD), HD)] = ri_v[pl.ds(pl.multiple_of(h * HD, HD), HD), :].T

    def attend(s, h):
        g = s * kvl + h // groups
        total = nn(vta[g], wb[s * hl + h]) + nn(pta[g], fq[s * hl + h])
        out = total[0:HD] * (1.0 / total[HD:HD + 1])
        ssq[s] += jnp.sum((out * out).reshape(HD // 16, 16, BLK), axis=0)
        scale = gcol[h]
        att[s, pl.ds(pl.multiple_of(h * HD, HD), HD), :] = jnp.concatenate(
            [out[:, 0:HD] * scale, out[:, HD:] * scale], axis=1).astype(bf16)

    def loop(start, stop, step, body):
        def trip(i, _):
            for j in range(step):
                body(start + i * step + j)
            return 0
        lax.fori_loop(0, (stop - start) // step, trip, 0)

    def body0(h):
        features(0, h)
        prepare(h)

    loop(0, hl, 2, body0)
    loads[6].wait()

    def wait1(i, _):
        arrival(send_e, recv_e, s1, r1, i).wait_recv()
        return 0

    lax.fori_loop(1, nc, wait1, 0)

    def scan(i, total):
        send_p[i] = total.astype(bf16)
        return total + recv_e[i].astype(f32)

    lax.fori_loop(0, nc, scan, jnp.zeros(send_p.shape[1:], f32))

    def start2(i, _):
        exchange(send_p, recv_p, s2, r2, i).start()
        return 0

    lax.fori_loop(1, nc, start2, 0)
    recv_p[mc] = send_p[mc]

    loop(0, hl, 2, lambda h: features(1, h))

    def wait2(i, _):
        arrival(send_p, recv_p, s2, r2, i).wait_recv()
        return 0

    lax.fori_loop(1, nc, wait2, 0)
    for i in range(SEQS * kvl):
        for p in range(per):
            pta[i, p * rows:(p + 1) * rows, :] = recv_p[i * per + p, :, 0:2 * HD]
        sums = recv_p[i * per, 0:2, 2 * HD:].astype(f32)
        pta[i, HD:HD + 16, :] = jnp.broadcast_to(
            jnp.concatenate([sums[0:1], sums[1:2]], axis=1), (16, BLK)).astype(bf16)

    ssq[...] = jnp.zeros_like(ssq)

    def partner(s, i):
        return lax.rem(mz + i, nz)

    def scatter(s, i):
        to = lax.rem(mz + i, nz)
        return pltpu.make_async_remote_copy(
            src_ref=msg.at[s, to], dst_ref=got.at[s, i - 1], send_sem=s3.at[s, i], recv_sem=r3.at[s, i],
            device_id=(mc, to), device_id_type=MESH)

    def gather(s, i, at):
        to = lax.rem(mz + i, nz)
        return pltpu.make_async_remote_copy(
            src_ref=red.at[s, at], dst_ref=red.at[s, at], send_sem=s4.at[s, i], recv_sem=r4.at[s, i],
            device_id=(mc, to), device_id_type=MESH)

    def project(s):
        part[s] = nn(rit[...], att[s])
        for p in range(nz):
            msg[s, p, 0:rb, :] = part[s, p * rb:(p + 1) * rb, :].astype(bf16)
            msg[s, p, rb:, :] = ssq[s].astype(bf16)
        for i in range(1, nz):
            scatter(s, i).start()

    def reduce(s):
        for i in range(1, nz):
            scatter(s, i).wait_recv()
        total = part[s, pl.ds(pl.multiple_of(mz * rb, rb), rb), :]
        squares = ssq[s]
        for i in range(1, nz):
            total = total + got[s, i - 1, 0:rb, :].astype(f32)
            squares = squares + got[s, i - 1, rb:, :].astype(f32)
        factor = lax.rsqrt(jnp.sum(squares, axis=0, keepdims=True) / feats + 1e-05)
        red[s, mz] = (total * factor).astype(bf16)
        for i in range(1, nz):
            gather(s, i, mz).start()

    loop(0, hl, 2, lambda h: attend(0, h))
    project(0)
    loop(0, hl // 2, 2, lambda h: attend(1, h))
    reduce(0)
    loop(hl // 2, hl, 2, lambda h: attend(1, h))
    project(1)
    reduce(1)
    for s in range(SEQS):
        for i in range(1, nz):
            gather(s, i, lax.rem(mz + nz - i, nz)).wait_recv()
        for p in range(nz):
            out_ref[s, p * rb:(p + 1) * rb, :] = red[s, p]

    def drain(i, _):
        exchange(send_e, recv_e, s1, r1, i).wait_send()
        exchange(send_p, recv_p, s2, r2, i).wait_send()
        return 0

    lax.fori_loop(1, nc, drain, 0)
    for s in range(SEQS):
        for i in range(1, nz):
            scatter(s, i).wait_send()
            gather(s, i, mz).wait_send()


def attention(nc, nz, q, k, v, qm, km, gain, ri):
    hl, kvl, rank = qm.shape[0], km.shape[0], ri.shape[1]
    rows = SEQS * kvl * HD // nc
    rb = rank // nz
    states = SEQS * kvl
    vm, dma = pltpu.VMEM, pltpu.SemaphoreType.DMA
    hbm = pl.BlockSpec(memory_space=pl.ANY)
    vmem = pl.BlockSpec(memory_space=pltpu.VMEM)
    return pl.pallas_call(
        functools.partial(kernel, nc, nz, float(nz * hl * HD)),
        out_shape=jax.ShapeDtypeStruct((SEQS, rank, BLK), bf16),
        in_specs=[hbm, hbm, hbm, hbm, hbm, vmem, hbm],
        out_specs=vmem,
        scratch_shapes=[
            vm(q.shape, bf16), vm(k.shape, bf16), vm(v.shape, bf16), vm(qm.shape, bf16),
            vm(km.shape, bf16), vm(ri.shape, bf16), vm((rank, hl * HD), bf16), vm((hl, HD, HD), f32),
            vm((states, BLK, 2 * HD), bf16), vm((states, HD + 16, BLK), bf16), vm((states, HD + 16, 2 * HD), bf16),
            vm((SEQS * hl, 2 * HD, BLK), bf16), vm((SEQS * hl, BLK, BLK), bf16),
            vm((SEQS, hl * HD, BLK), bf16), vm((SEQS, 16, BLK), f32), vm((SEQS, rank, BLK), f32),
            vm((nc, rows, 3 * HD), bf16), vm((nc, rows, 3 * HD), bf16),
            vm((nc, rows, 3 * HD), bf16), vm((nc, rows, 3 * HD), bf16),
            vm((SEQS, nz, rb + 16, BLK), bf16), vm((SEQS, nz - 1, rb + 16, BLK), bf16),
            vm((SEQS, nz, rb, BLK), bf16),
            dma((7,)), dma((nc,)), dma((nc,)), dma((nc,)), dma((nc,)),
            dma((SEQS, nz)), dma((SEQS, nz)), dma((SEQS, nz)), dma((SEQS, nz)),
        ],
        compiler_params=pltpu.CompilerParams(
            collective_id=0, has_side_effects=True, vmem_limit_bytes=60 * 2**20),
        name="attention",
    )(q, k, v, qm, km, gain, ri)


def solution(mesh):
    nc, nz = mesh.shape["ctx"], mesh.shape["head"]

    def shards(queries, key_input, values, query_map, key_map, out_gain, rank_in, rank_out):
        reduced = attention(nc, nz, queries, key_input, values, query_map, key_map,
                            out_gain.reshape(1, -1), rank_in)
        result = lax.dot_general(reduced, rank_out, (((1,), (0,)), ((), ())), preferred_element_type=f32)
        return result.astype(bf16)

    in_specs = (
        P(None, "ctx", "head"),
        P(None, "ctx", "head"),
        P(None, "ctx", "head"),
        P("head", None, None),
        P("head", None, None),
        P("head"),
        P("head", None),
        P(None, "head"),
    )
    out_specs = P(None, "ctx", "head")
    return jax.shard_map(shards, mesh=mesh, in_specs=in_specs, out_specs=out_specs, check_vma=False)
```

time: 190 us -> 64.1 us (0.34)
  blocking collectives: 67.2 us -> 0 us
  Pallas kernels: 0 us -> 55.9 us
  matrix products: 48.2 us -> 6.74 us
  local copies, waits for them, and re-layouts: 32.7 us -> 1.31 us
  other arithmetic: 27.9 us -> 0 us
  between operations: 13.5 us -> 0.01 us
    pallas_call x0 -> x1, Pallas kernels: none -> 55.9 us  [attention(): pl.pallas_call(functools.partial(kernel, nc, nz, float(nz * hl * HD)), ou...]
    psum x2 -> x0, blocking collectives: 41.9 us -> none  [the longest x1 29.8 us: shards(): reduced = lax.psum(partial_rank, 'head').astype(jnp.bfloat16)]
    dot_general x8 -> x1, matrix products: 45.4 us -> 6.74 us  [shards(): lax.dot_general(reduced, rank_out, (((1,), (0,)), ((), ())), preferred_el...]
    all_gather x1 -> x0, blocking collectives: 25.3 us -> none  [shards(): lax.all_gather(key_sums[None], 'ctx', axis=0, tiled=True)]
    sub x2 -> x0, other arithmetic: 14 us -> none  [the longest x1 9.3 us: feature_pair(): jax.nn.softmax(-scores, axis=-1)]
    div x1 -> x0, local copies, waits for them, and re-layouts: 10.3 us -> none  [shards(): attended = (local_num + carried_num) / (local_den + carried_den)[..., None]]
    reshape x2 -> x1, local copies, waits for them, and re-layouts: 10.4 us -> 1.31 us  [shards(): out_gain.reshape(1, -1)]
    reduce_sum x3 -> x0, other arithmetic: 7.84 us -> none  [the longest x1 7.49 us: shards(): jnp.sum(jnp.where(lower[:, None, None, None, None], pieces[0], 0.0), axis=0)]
  transfers between devices with their start and end apart: 1 -> 0, of which waited for: 0 -> 0; matrix products, arithmetic and copies ran while one was open for 26% -> 0% of each run, Pallas kernels for 0% -> 0%
where the time goes in v1:
time: 64.1 us; the launch traced here: 63.9 us
  Pallas kernels  55.9 us (87%)
  matrix products  6.74 us (11%)
  local copies, waits for them, and re-layouts  1.31 us (2%)
    pallas_call x1, Pallas kernels, attention(): pl.pallas_call(functools.partial(kernel, nc, nz, float(nz * hl * HD)), ou...  55.9 us
    dot_general x1, matrix products, shards(): lax.dot_general(reduced, rank_out, (((1,), (0,)), ((), ())), preferred_el...  6.74 us
    reshape x1, local copies, waits for them, and re-layouts, shards(): out_gain.reshape(1, -1)  1.31 us

profile of v1, /device:TPU:0, one launch (start us, length us, event | category | flops | bytes accessed | tf_op | source)
XLA Modules:
  0.0 63.9 jit_solution(8604011477277342364)
XLA Ops:
  0.0 1.3 %reshape.3.gain_ref = bf16[1,4096]{1,0:T(2,128)(2,1)} reshape(bf16[4096]{0:T(1024)(128)(2,1)} %param.13) | data formatting | bytes 16384 | tf_op jit(solution)/shard_map/reshape | solution.py:275
  1.3 55.9 %attention.1 = bf16[2,512,256]{2,1,0:T(8,128)(2,1)} custom-call(bf16[2,256,4096]{2,1,0:T(8,128)(2,1)} %q_hbm.1, bf16[2,256,256]{2,1,0:T(8,128)(2,1)} %k_hbm.1, bf16[2,256,256]{2,1,0:T(8,128)(2,1)} %v_hbm.1, bf16[32,128,128]{2,1,0:T(8,128)(2,1)} %qm_hbm.1, bf16[2,128,128]{2,1,0:T(8,128)(2,1)} %km_hbm.1, bf16[1,4096]{1,0:T(2,128)(2,1)} %reshape.3.gain_ref, ...), custom_call_target="tpu_custom_call" | custom-call | tf_op jit(solution)/shard_map/attention/pallas_call | solution.py:246
  57.2 6.7 %convolution_convert_fusion = bf16[2,256,4096]{2,1,0:T(8,128)(2,1)} fusion(bf16[2,512,256]{2,1,0:T(8,128)(2,1)} %attention.1, bf16[512,4096]{1,0:T(8,128)(2,1)} %param.15), kind=kOutput, calls=%fused_computation | convolution fusion | flops 2149580800 | bytes 8912896 | tf_op jit(solution)/shard_map/dot_general | solution.py:276

commit v2 on v1

v2 whole, which is shorter than its diff:
```python
import functools

import jax
import jax.numpy as jnp
from jax import lax
from jax.experimental import pallas as pl
from jax.experimental.pallas import tpu as pltpu
from jax.sharding import PartitionSpec as P

HD = 128
BLK = 256
SEQS = 2
ST, AT = 8, 8
VLIM = 59
LOG2E = 1.4426950408889634
MESH = pl.DeviceIdType.MESH
bf16, f32 = jnp.bfloat16, jnp.float32


def nn(a, b):
    return jnp.dot(a, b, preferred_element_type=f32)


def tt(a, b):
    return lax.dot_general(a, b, (((0,), (1,)), ((), ())), preferred_element_type=f32)


def exps(scaled):
    pos = jnp.exp2(scaled - jnp.max(scaled, axis=0, keepdims=True))
    neg = jnp.exp2(jnp.min(scaled, axis=0, keepdims=True) - scaled)
    return pos, neg, jnp.sum(pos, axis=0, keepdims=True), jnp.sum(neg, axis=0, keepdims=True)


def kernel(nc, nz, feats, q_hbm, k_hbm, v_hbm, qm_hbm, km_hbm, gain_ref, ri_hbm, out_ref,
           q_v, k_v, v_v, qm_v, km_v, ri_v, rit, gcol, fk, vta, pta, att, ssq, part,
           send_e, recv_e, send_p, recv_p, msg, got, red,
           tri, raw, tot, in_sem, s1, r1, s2, r2, s3, r3, s4, r4, *per_head):
    fq, wb = per_head[:len(per_head) // 2], per_head[len(per_head) // 2:]
    hl, kvl = qm_v.shape[0], km_v.shape[0]
    groups = hl // kvl
    rank = ri_v.shape[1]
    rb = rank // nz
    rows = send_e.shape[1]
    per = HD // rows
    mc, mz = lax.axis_index("ctx"), lax.axis_index("head")

    loads = [(k_hbm, k_v), (v_hbm, v_v), (km_hbm, km_v), (qm_hbm, qm_v),
             (q_hbm.at[0], q_v.at[0]), (ri_hbm, ri_v), (q_hbm.at[1], q_v.at[1])]
    loads = [pltpu.make_async_copy(a, b, in_sem.at[i]) for i, (a, b) in enumerate(loads)]
    for load in loads:
        load.start()

    barrier = pltpu.get_barrier_semaphore()

    def greet_ctx(i, _):
        pl.semaphore_signal(barrier, inc=1, device_id=(lax.rem(mc + i, nc), mz), device_id_type=MESH)
        return 0

    lax.fori_loop(1, nc, greet_ctx, 0)
    for i in range(1, nz):
        pl.semaphore_signal(barrier, inc=1, device_id=(mc, lax.rem(mz + i, nz)), device_id_type=MESH)

    for load in loads[:3]:
        load.wait()
    first = lax.broadcasted_iota(jnp.int32, (rows, HD), 0) == 0
    for s in range(SEQS):
        for g in range(kvl):
            i = s * kvl + g
            lanes = slice(g * HD, (g + 1) * HD)
            pos, neg, zp, zn = exps(tt(km_v[g], k_v[s, :, lanes]) * LOG2E)
            feat = jnp.concatenate([pos * (1.0 / zp), neg * (1.0 / zn)], axis=0).astype(bf16)
            fk[i] = feat.T
            vta[i, 0:HD, :] = v_v[s, :, lanes].T
            vta[i, HD:HD + 16, :] = jnp.ones((16, BLK), bf16)
            state = nn(vta[i], fk[i])
            for p in range(per):
                j = i * per + p
                send_e[j, :, 0:2 * HD] = state[p * rows:(p + 1) * rows].astype(bf16)
                send_e[j, :, 2 * HD:] = jnp.where(
                    first, state[HD:HD + 1, 0:HD], state[HD:HD + 1, HD:2 * HD]).astype(bf16)

    pl.semaphore_wait(barrier, nc - 1 + nz - 1)

    def exchange(src, dst, ssem, rsem, i):
        to = lax.rem(mc + i, nc)
        return pltpu.make_async_remote_copy(
            src_ref=src.at[to], dst_ref=dst.at[mc], send_sem=ssem, recv_sem=rsem,
            device_id=(to, mz), device_id_type=MESH)

    def arrivals(src, dst, ssem, rsem):
        return pltpu.make_async_remote_copy(
            src_ref=src.at[pl.ds(0, nc - 1)], dst_ref=dst.at[pl.ds(0, nc - 1)], send_sem=ssem, recv_sem=rsem,
            device_id=(lax.rem(mc + 1, nc), mz), device_id_type=MESH)

    for i in range(1, nc):
        exchange(send_e, recv_e, s1, r1, i).start()
    recv_e[mc] = send_e[mc]

    for load in loads[3:6]:
        load.wait()

    tri[...] = (lax.broadcasted_iota(jnp.int32, (HD, HD), 0)
                <= lax.broadcasted_iota(jnp.int32, (HD, HD), 1)).astype(f32).astype(bf16)

    ST, AT = raw.shape[0], tot.shape[0]

    def joined(ref, i):
        return jnp.concatenate([ref[i, 0], ref[i, 1]], axis=1)

    def lanes_of(h):
        return pl.ds(pl.multiple_of(h * HD, HD), HD)

    def dots(s, i, j):
        h = i * ST + j
        raw[j] = tt(qm_v[h], q_v[s, :, lanes_of(h)]) * LOG2E

    def features(s, i, j):
        at = s * (hl // ST) + i
        for c in range(BLK // HD):
            pos, neg, zp, zn = exps(raw[j, :, c * HD:(c + 1) * HD])
            fq[j][at, c, 0:HD, :] = pos.astype(bf16)
            fq[j][at, c, HD:, :] = (neg * (zp / zn)).astype(bf16)

    def weigh(s, i, j):
        at = s * (hl // ST) + i
        score = nn(fk[s * kvl + (i * ST + j) // groups], joined(fq[j], at))
        wb[j][at, 0, 0:HD, :] = score[0:HD, 0:HD].astype(bf16) * tri[...]
        wb[j][at, 1, 0:HD, :] = score[0:HD, HD:].astype(bf16)
        wb[j][at, 0, HD:, :] = jnp.zeros((HD, HD), bf16)
        wb[j][at, 1, HD:, :] = score[HD:, HD:].astype(bf16) * tri[...]

    def prepare(i, j):
        at = lanes_of(i * ST + j)
        gcol[i * ST + j] = jnp.broadcast_to(gain_ref[0:1, at].astype(f32), (HD, HD)).T
        rit[:, at] = ri_v[at, :].T

    def attend(s, i, j):
        g = s * kvl + (i * AT + j) // groups
        at = s * (hl // ST) + i * (AT // ST) + j // ST
        tot[j] = nn(vta[g], joined(wb[j % ST], at)) + nn(pta[g], joined(fq[j % ST], at))

    def divide(s, i, j):
        h = i * AT + j
        out = tot[j, 0:HD] * (1.0 / tot[j, HD:HD + 1])
        ssq[s] += jnp.sum((out * out).reshape(HD // 16, 16, BLK), axis=0)
        scale = gcol[h]
        att[s, lanes_of(h), :] = jnp.concatenate(
            [out[:, 0:HD] * scale, out[:, HD:] * scale], axis=1).astype(bf16)

    def heads(step, stages, extra=None):
        depth, count = len(stages) - 1, hl // step
        last = depth + (extra is not None)

        def trip(i, live):
            if extra is not None and last in live:
                extra(i - last)
            for j in range(step):
                for k in range(depth, -1, -1):
                    if k in live:
                        stages[k](i - k, j)

        for i in range(last):
            trip(i, range(0, i + 1))

        def run(i, _):
            trip(i, range(last + 1))
            return 0

        lax.fori_loop(last, count, run, 0)
        for i in range(count, count + last):
            trip(i, range(i - count + 1, last + 1))

    heads(ST, [lambda i, j: dots(0, i, j), lambda i, j: (features(0, i, j), prepare(i, j)),
               lambda i, j: weigh(0, i, j)])
    loads[6].wait()

    arrivals(send_e, recv_e, s1, r1).wait_recv()

    def scan(i, total):
        send_p[i] = total.astype(bf16)
        return total + recv_e[i].astype(f32)

    lax.fori_loop(0, nc, scan, jnp.zeros(send_p.shape[1:], f32))

    for i in range(1, nc):
        exchange(send_p, recv_p, s2, r2, i).start()
    recv_p[mc] = send_p[mc]

    heads(ST, [functools.partial(f, 1) for f in (dots, features, weigh)])

    arrivals(send_p, recv_p, s2, r2).wait_recv()
    for i in range(SEQS * kvl):
        for p in range(per):
            pta[i, p * rows:(p + 1) * rows, :] = recv_p[i * per + p, :, 0:2 * HD]
        sums = recv_p[i * per, 0:2, 2 * HD:].astype(f32)
        pta[i, HD:HD + 16, :] = jnp.broadcast_to(
            jnp.concatenate([sums[0:1], sums[1:2]], axis=1), (16, BLK)).astype(bf16)

    ssq[...] = jnp.zeros_like(ssq)

    def partner(s, i):
        return lax.rem(mz + i, nz)

    def scatter(s, i):
        to = lax.rem(mz + i, nz)
        return pltpu.make_async_remote_copy(
            src_ref=msg.at[s, i - 1], dst_ref=got.at[s, i - 1], send_sem=s3.at[s, i], recv_sem=r3.at[s, i],
            device_id=(mc, to), device_id_type=MESH)

    def gather(s, i, at):
        to = lax.rem(mz + i, nz)
        return pltpu.make_async_remote_copy(
            src_ref=red.at[s, at], dst_ref=red.at[s, at], send_sem=s4.at[s, i], recv_sem=r4.at[s, i],
            device_id=(mc, to), device_id_type=MESH)

    def project(s):
        for i in (2, 1, 3, 0) if nz == 4 else range(nz - 1, -1, -1):
            to = lax.rem(mz + i, nz)
            block = nn(rit[pl.ds(pl.multiple_of(to * rb, rb), rb), :], att[s])
            if i == 0:
                part[s] = block
            else:
                msg[s, i - 1, 0:rb, :] = block.astype(bf16)
                msg[s, i - 1, rb:, :] = ssq[s].astype(bf16)
                scatter(s, i).start()

    def reduce(s):
        for i in range(1, nz):
            scatter(s, i).wait_recv()
        total = part[s]
        squares = ssq[s]
        for i in range(1, nz):
            total = total + got[s, i - 1, 0:rb, :].astype(f32)
            squares = squares + got[s, i - 1, rb:, :].astype(f32)
        factor = lax.rsqrt(jnp.sum(squares, axis=0, keepdims=True) / feats + 1e-05)
        red[s, mz] = (total * factor).astype(bf16)
        for i in range(1, nz):
            gather(s, i, mz).start()

    heads(AT, [functools.partial(f, 0) for f in (attend, divide)])
    project(0)
    heads(AT, [functools.partial(f, 1) for f in (attend, divide)])
    reduce(0)
    project(1)
    reduce(1)
    for s in range(SEQS):
        for i in range(1, nz):
            gather(s, i, lax.rem(mz + nz - i, nz)).wait_recv()
        for p in range(nz):
            out_ref[s, :, p * rb:(p + 1) * rb] = red[s, p].T

    arrivals(send_e, recv_e, s1, r1).wait_send()
    arrivals(send_p, recv_p, s2, r2).wait_send()
    for s in range(SEQS):
        for i in range(1, nz):
            scatter(s, i).wait_send()
            gather(s, i, mz).wait_send()


def attention(nc, nz, q, k, v, qm, km, gain, ri):
    hl, kvl, rank = qm.shape[0], km.shape[0], ri.shape[1]
    rows = SEQS * kvl * HD // nc
    rb = rank // nz
    states = SEQS * kvl
    st, at = min(ST, hl), min(AT, hl)
    vm, dma = pltpu.VMEM, pltpu.SemaphoreType.DMA
    hbm = pl.BlockSpec(memory_space=pltpu.HBM)
    vmem = pl.BlockSpec(memory_space=pltpu.VMEM)
    return pl.pallas_call(
        functools.partial(kernel, nc, nz, float(nz * hl * HD)),
        out_shape=jax.ShapeDtypeStruct((SEQS, BLK, rank), bf16),
        in_specs=[hbm, hbm, hbm, hbm, hbm, vmem, hbm],
        out_specs=vmem,
        scratch_shapes=[
            vm(q.shape, bf16), vm(k.shape, bf16), vm(v.shape, bf16), vm(qm.shape, bf16),
            vm(km.shape, bf16), vm(ri.shape, bf16), vm((rank, hl * HD), bf16), vm((hl, HD, HD), f32),
            vm((states, BLK, 2 * HD), bf16), vm((states, HD + 16, BLK), bf16), vm((states, HD + 16, 2 * HD), bf16),
            vm((SEQS, hl * HD, BLK), bf16), vm((SEQS, 16, BLK), f32), vm((SEQS, rb, BLK), f32),
            vm((nc, rows, 3 * HD), bf16), vm((nc, rows, 3 * HD), bf16),
            vm((nc, rows, 3 * HD), bf16), vm((nc, rows, 3 * HD), bf16),
            vm((SEQS, nz - 1, rb + 16, BLK), bf16), vm((SEQS, nz - 1, rb + 16, BLK), bf16),
            vm((SEQS, nz, rb, BLK), bf16), vm((HD, HD), bf16),
            vm((st, HD, BLK), f32), vm((at, HD + 16, BLK), f32),
            dma((7,)), dma, dma, dma, dma,
            dma((SEQS, nz)), dma((SEQS, nz)), dma((SEQS, nz)), dma((SEQS, nz)),
        ] + [vm((SEQS * hl // st, 2, 2 * HD, HD), bf16)] * st + [
            vm((SEQS * hl // st, 2, BLK, HD), bf16)] * st + [
        ],
        compiler_params=pltpu.CompilerParams(
            collective_id=0, has_side_effects=True, vmem_limit_bytes=VLIM * 2**20),
        name="attention",
    )(q, k, v, qm, km, gain, ri)


def solution(mesh):
    nc, nz = mesh.shape["ctx"], mesh.shape["head"]

    def shards(queries, key_input, values, query_map, key_map, out_gain, rank_in, rank_out):
        reduced = attention(nc, nz, queries, key_input, values, query_map, key_map,
                            out_gain.reshape(1, -1), rank_in)
        return jnp.einsum('str,rn->stn', reduced, rank_out, preferred_element_type=f32).astype(bf16)

    in_specs = (
        P(None, "ctx", "head"),
        P(None, "ctx", "head"),
        P(None, "ctx", "head"),
        P("head", None, None),
        P("head", None, None),
        P("head"),
        P("head", None),
        P(None, "head"),
    )
    out_specs = P(None, "ctx", "head")
    return jax.shard_map(shards, mesh=mesh, in_specs=in_specs, out_specs=out_specs, check_vma=False)
```

time: 64.1 us -> 54.6 us (0.85)
  Pallas kernels: 55.9 us -> 47.7 us
  matrix products: 6.74 us -> 5.41 us
    pallas_call x1, Pallas kernels: 55.9 us -> 47.7 us  [attention(): pl.pallas_call(functools.partial(kernel, nc, nz, float(nz * hl * HD)), ou...]
    dot_general x1, matrix products: 6.74 us -> 5.41 us  [shards(): jnp.einsum('str,rn->stn', reduced, rank_out, preferred_element_type=f32)]
where the time goes in v2:
time: 54.6 us; the launch traced here: 54.4 us
  Pallas kernels  47.7 us (87%)
  matrix products  5.41 us (10%)
  local copies, waits for them, and re-layouts  1.31 us (2%)
    pallas_call x1, Pallas kernels, attention(): pl.pallas_call(functools.partial(kernel, nc, nz, float(nz * hl * HD)), ou...  47.7 us
    dot_general x1, matrix products, shards(): jnp.einsum('str,rn->stn', reduced, rank_out, preferred_element_type=f32)  5.41 us
    reshape x1, local copies, waits for them, and re-layouts, shards(): out_gain.reshape(1, -1)  1.31 us

profile of v2, /device:TPU:0, one launch (start us, length us, event | category | flops | bytes accessed | tf_op | source)
XLA Modules:
  0.0 54.4 jit_solution(4648437241142891684)
XLA Ops:
  0.0 1.3 %reshape.3.gain_ref = bf16[1,4096]{1,0:T(2,128)(2,1)} reshape(bf16[4096]{0:T(1024)(128)(2,1)} %param.13) | data formatting | bytes 16384 | tf_op jit(solution)/shard_map/reshape | solution.py:300
  1.3 0.0 copy-start
  1.3 47.7 %attention.1 = bf16[2,256,512]{2,1,0:T(8,128)(2,1)} custom-call(bf16[2,256,4096]{2,1,0:T(8,128)(2,1)} %q_hbm.1, bf16[2,256,256]{2,1,0:T(8,128)(2,1)} %k_hbm.1, bf16[2,256,256]{2,1,0:T(8,128)(2,1)} %v_hbm.1, bf16[32,128,128]{2,1,0:T(8,128)(2,1)} %qm_hbm.1, bf16[2,128,128]{2,1,0:T(8,128)(2,1)} %km_hbm.1, bf16[1,4096]{1,0:T(2,128)(2,1)} %reshape.3.gain_ref, ...), custom_call_target="tpu_custom_call" | custom-call | tf_op jit(solution)/shard_map/attention/pallas_call | solution.py:269
  49.0 0.0 copy-done
  49.0 5.4 %convolution_convert_fusion = bf16[2,256,4096]{2,1,0:T(8,128)(2,1)} fusion(bf16[2,256,512]{2,1,0:T(8,128)(2,1)} %attention.1, bf16[512,4096]{1,0:T(8,128)(2,1)S(1)} %copy-done), kind=kOutput, calls=%fused_computation | convolution fusion | flops 2149580800 | bytes 8912896 | tf_op jit(solution)/shard_map/str,rn->stn/dot_general | solution.py:301
Async XLA Ops:
  1.3 47.7 %copy-start = (bf16[512,4096]{1,0:T(8,128)(2,1)S(1)}, bf16[512,4096]{1,0:T(8,128)(2,1)}, u32[]{:S(2)}) copy-start(bf16[512,4096]{1,0:T(8,128)(2,1)} %param.15) | copy-start | bytes 12582916

commit v3 on v2

--- a/solution.py
+++ b/solution.py
@@ -12,6 +12,7 @@
 SEQS = 2
 ST, AT = 8, 8
 VLIM = 59
+OUT_TILES = 4
 LOG2E = 1.4426950408889634
 MESH = pl.DeviceIdType.MESH
 bf16, f32 = jnp.bfloat16, jnp.float32
@@ -31,8 +32,8 @@
     return pos, neg, jnp.sum(pos, axis=0, keepdims=True), jnp.sum(neg, axis=0, keepdims=True)
 
 
-def kernel(nc, nz, feats, q_hbm, k_hbm, v_hbm, qm_hbm, km_hbm, gain_ref, ri_hbm, out_ref,
-           q_v, k_v, v_v, qm_v, km_v, ri_v, rit, gcol, fk, vta, pta, att, ssq, part,
+def kernel(nc, nz, feats, q_hbm, k_hbm, v_hbm, qm_hbm, km_hbm, gain_ref, ri_hbm, ro_hbm, out_ref,
+           q_v, k_v, v_v, qm_v, km_v, ri_v, ro_v, rit, gcol, gains, fk, vta, pta, att, ssq, part,
            send_e, recv_e, send_p, recv_p, msg, got, red,
            tri, raw, tot, in_sem, s1, r1, s2, r2, s3, r3, s4, r4, *per_head):
     fq, wb = per_head[:len(per_head) // 2], per_head[len(per_head) // 2:]
@@ -45,11 +46,12 @@
     mc, mz = lax.axis_index("ctx"), lax.axis_index("head")
 
     loads = [(k_hbm, k_v), (v_hbm, v_v), (km_hbm, km_v), (qm_hbm, qm_v),
-             (q_hbm.at[0], q_v.at[0]), (ri_hbm, ri_v), (q_hbm.at[1], q_v.at[1])]
+             (q_hbm.at[0], q_v.at[0]), (ri_hbm, ri_v), (q_hbm.at[1], q_v.at[1]), (ro_hbm, ro_v)]
     loads = [pltpu.make_async_copy(a, b, in_sem.at[i]) for i, (a, b) in enumerate(loads)]
     for load in loads:
         load.start()
 
+    gains[...] = gain_ref[...].astype(f32)
     barrier = pltpu.get_barrier_semaphore()
 
     def greet_ctx(i, _):
@@ -131,7 +133,7 @@
 
     def prepare(i, j):
         at = lanes_of(i * ST + j)
-        gcol[i * ST + j] = jnp.broadcast_to(gain_ref[0:1, at].astype(f32), (HD, HD)).T
+        gcol[i * ST + j] = jnp.broadcast_to(gains[pl.ds(i * ST + j, 1), :], (HD, HD)).T
         rit[:, at] = ri_v[at, :].T
 
     def attend(s, i, j):
@@ -237,18 +239,24 @@
         for i in range(1, nz):
             gather(s, i, mz).start()
 
+    def expand(s):
+        for i in range(1, nz):
+            gather(s, i, lax.rem(mz + nz - i, nz)).wait_recv()
+        lhs = jnp.concatenate([red[s, p].T for p in range(nz)], axis=1)
+        tile = out_ref.shape[2] // OUT_TILES
+        for n in range(OUT_TILES):
+            cols = slice(n * tile, (n + 1) * tile)
+            out_ref[s, :, cols] = nn(lhs, ro_v[:, cols]).astype(bf16)
+
     heads(AT, [functools.partial(f, 0) for f in (attend, divide)])
     project(0)
     heads(AT, [functools.partial(f, 1) for f in (attend, divide)])
     reduce(0)
     project(1)
+    loads[7].wait()
+    expand(0)
     reduce(1)
-    for s in range(SEQS):
-        for i in range(1, nz):
-            gather(s, i, lax.rem(mz + nz - i, nz)).wait_recv()
-        for p in range(nz):
-            out_ref[s, :, p * rb:(p + 1) * rb] = red[s, p].T
-
+    expand(1)
     arrivals(send_e, recv_e, s1, r1).wait_send()
     arrivals(send_p, recv_p, s2, r2).wait_send()
     for s in range(SEQS):
@@ -257,7 +265,7 @@
             gather(s, i, mz).wait_send()
 
 
-def attention(nc, nz, q, k, v, qm, km, gain, ri):
+def attention(nc, nz, q, k, v, qm, km, gain, ri, ro):
     hl, kvl, rank = qm.shape[0], km.shape[0], ri.shape[1]
     rows = SEQS * kvl * HD // nc
     rb = rank // nz
@@ -268,12 +276,13 @@
     vmem = pl.BlockSpec(memory_space=pltpu.VMEM)
     return pl.pallas_call(
         functools.partial(kernel, nc, nz, float(nz * hl * HD)),
-        out_shape=jax.ShapeDtypeStruct((SEQS, BLK, rank), bf16),
-        in_specs=[hbm, hbm, hbm, hbm, hbm, vmem, hbm],
-        out_specs=vmem,
+        out_shape=pltpu.VMEM(q.shape, bf16),
+        in_specs=[hbm, hbm, hbm, hbm, hbm, vmem, hbm, hbm],
+        out_specs=pl.BlockSpec(memory_space=pltpu.VMEM),
         scratch_shapes=[
             vm(q.shape, bf16), vm(k.shape, bf16), vm(v.shape, bf16), vm(qm.shape, bf16),
-            vm(km.shape, bf16), vm(ri.shape, bf16), vm((rank, hl * HD), bf16), vm((hl, HD, HD), f32),
+            vm(km.shape, bf16), vm(ri.shape, bf16), vm(ro.shape, bf16),
+            vm((rank, hl * HD), bf16), vm((hl, HD, HD), f32), vm((hl, HD), f32),
             vm((states, BLK, 2 * HD), bf16), vm((states, HD + 16, BLK), bf16), vm((states, HD + 16, 2 * HD), bf16),
             vm((SEQS, hl * HD, BLK), bf16), vm((SEQS, 16, BLK), f32), vm((SEQS, rb, BLK), f32),
             vm((nc, rows, 3 * HD), bf16), vm((nc, rows, 3 * HD), bf16),
@@ -281,7 +290,7 @@
             vm((SEQS, nz - 1, rb + 16, BLK), bf16), vm((SEQS, nz - 1, rb + 16, BLK), bf16),
             vm((SEQS, nz, rb, BLK), bf16), vm((HD, HD), bf16),
             vm((st, HD, BLK), f32), vm((at, HD + 16, BLK), f32),
-            dma((7,)), dma, dma, dma, dma,
+            dma((8,)), dma, dma, dma, dma,
             dma((SEQS, nz)), dma((SEQS, nz)), dma((SEQS, nz)), dma((SEQS, nz)),
         ] + [vm((SEQS * hl // st, 2, 2 * HD, HD), bf16)] * st + [
             vm((SEQS * hl // st, 2, BLK, HD), bf16)] * st + [
@@ -289,16 +298,15 @@
         compiler_params=pltpu.CompilerParams(
             collective_id=0, has_side_effects=True, vmem_limit_bytes=VLIM * 2**20),
         name="attention",
-    )(q, k, v, qm, km, gain, ri)
+    )(q, k, v, qm, km, gain, ri, ro)
 
 
 def solution(mesh):
     nc, nz = mesh.shape["ctx"], mesh.shape["head"]
 
     def shards(queries, key_input, values, query_map, key_map, out_gain, rank_in, rank_out):
-        reduced = attention(nc, nz, queries, key_input, values, query_map, key_map,
-                            out_gain.reshape(1, -1), rank_in)
-        return jnp.einsum('str,rn->stn', reduced, rank_out, preferred_element_type=f32).astype(bf16)
+        return attention(nc, nz, queries, key_input, values, query_map, key_map,
+                         out_gain.reshape(-1, HD), rank_in, rank_out)
 
     in_specs = (
         P(None, "ctx", "head"),

time: 54.6 us -> 50.1 us (0.918)
  matrix products: 5.41 us -> 0 us
  local copies, waits for them, and re-layouts: 1.31 us -> 2.02 us
    dot_general x1 -> x0, matrix products: 5.41 us -> none  [shards(): jnp.einsum('str,rn->stn', reduced, rank_out, preferred_element_type=f32)]
    unnamed x2 -> x1, local copies, waits for them, and re-layouts: 0.01 us -> 2.02 us
    reshape x1 -> x0, local copies, waits for them, and re-layouts: 1.31 us -> none  [shards(): out_gain.reshape(1, -1)]
where the time goes in v3:
time: 50.1 us; the launch traced here: 50 us
  Pallas kernels  47.9 us (96%)
  local copies, waits for them, and re-layouts  2.02 us (4%)
    pallas_call x1, Pallas kernels, attention(): pl.pallas_call(functools.partial(kernel, nc, nz, float(nz * hl * HD)), ou...  47.9 us
    unnamed x1, local copies, waits for them, and re-layouts  2.02 us

profile of v3, /device:TPU:0, one launch (start us, length us, event | category | flops | bytes accessed | tf_op | source)
XLA Modules:
  0.0 50.0 jit_solution(203543535874307176)
XLA Ops:
  0.0 47.9 %attention.1 = bf16[2,256,4096]{2,1,0:T(8,128)(2,1)S(1)} custom-call(bf16[2,256,4096]{2,1,0:T(8,128)(2,1)} %q_hbm.1, bf16[2,256,256]{2,1,0:T(8,128)(2,1)} %k_hbm.1, bf16[2,256,256]{2,1,0:T(8,128)(2,1)} %v_hbm.1, bf16[32,128,128]{2,1,0:T(8,128)(2,1)} %qm_hbm.1, bf16[2,128,128]{2,1,0:T(8,128)(2,1)} %km_hbm.1, bf16[32,128]{1,0:T(8,128)(2,1)} %bitcast.1, ...), custom_call_target="tpu_custom_call" | custom-call | tf_op jit(solution)/shard_map/attention/pallas_call | solution.py:277
  47.9 2.0 %copy.10 = bf16[2,256,4096]{2,1,0:T(8,128)(2,1)} copy(bf16[2,256,4096]{2,1,0:T(8,128)(2,1)S(1)} %attention.1) | data formatting | bytes 8388608

commit v4 on v3

--- a/solution.py
+++ b/solution.py
@@ -10,7 +10,7 @@
 HD = 128
 BLK = 256
 SEQS = 2
-ST, AT = 8, 8
+ST = 8
 VLIM = 59
 OUT_TILES = 4
 LOG2E = 1.4426950408889634
@@ -35,8 +35,9 @@
 def kernel(nc, nz, feats, q_hbm, k_hbm, v_hbm, qm_hbm, km_hbm, gain_ref, ri_hbm, ro_hbm, out_ref,
            q_v, k_v, v_v, qm_v, km_v, ri_v, ro_v, rit, gcol, gains, fk, vta, pta, att, ssq, part,
            send_e, recv_e, send_p, recv_p, msg, got, red,
-           tri, raw, tot, in_sem, s1, r1, s2, r2, s3, r3, s4, r4, *per_head):
-    fq, wb = per_head[:len(per_head) // 2], per_head[len(per_head) // 2:]
+           tri, raw, tot, near, in_sem, s1, r1, s2, r2, s3, r3, s4, r4, *per_head):
+    n = len(per_head) // 3
+    fq, wb, loc = per_head[:n], per_head[n:2 * n], per_head[2 * n:]
     hl, kvl = qm_v.shape[0], km_v.shape[0]
     groups = hl // kvl
     rank = ri_v.shape[1]
@@ -104,7 +105,7 @@
     tri[...] = (lax.broadcasted_iota(jnp.int32, (HD, HD), 0)
                 <= lax.broadcasted_iota(jnp.int32, (HD, HD), 1)).astype(f32).astype(bf16)
 
-    ST, AT = raw.shape[0], tot.shape[0]
+    ST = raw.shape[0]
 
     def joined(ref, i):
         return jnp.concatenate([ref[i, 0], ref[i, 1]], axis=1)
@@ -136,39 +137,41 @@
         gcol[i * ST + j] = jnp.broadcast_to(gains[pl.ds(i * ST + j, 1), :], (HD, HD)).T
         rit[:, at] = ri_v[at, :].T
 
+    def local(s, i, j):
+        loc[j][i] = nn(vta[s * kvl + (i * ST + j) // groups], joined(wb[j], s * (hl // ST) + i))
+
     def attend(s, i, j):
-        g = s * kvl + (i * AT + j) // groups
-        at = s * (hl // ST) + i * (AT // ST) + j // ST
-        tot[j] = nn(vta[g], joined(wb[j % ST], at)) + nn(pta[g], joined(fq[j % ST], at))
+        tot[j] = loc[j][i] + nn(pta[s * kvl + (i * ST + j) // groups], joined(fq[j], s * (hl // ST) + i))
 
     def divide(s, i, j):
-        h = i * AT + j
+        h = i * ST + j
         out = tot[j, 0:HD] * (1.0 / tot[j, HD:HD + 1])
         ssq[s] += jnp.sum((out * out).reshape(HD // 16, 16, BLK), axis=0)
         scale = gcol[h]
         att[s, lanes_of(h), :] = jnp.concatenate(
             [out[:, 0:HD] * scale, out[:, HD:] * scale], axis=1).astype(bf16)
 
-    def heads(step, stages, extra=None):
-        depth, count = len(stages) - 1, hl // step
-        last = depth + (extra is not None)
+    def heads(step, stages, hook=None):
+        last, count = len(stages) - 1, hl // step
 
         def trip(i, live):
-            if extra is not None and last in live:
-                extra(i - last)
             for j in range(step):
-                for k in range(depth, -1, -1):
+                for k in range(last, -1, -1):
                     if k in live:
                         stages[k](i - k, j)
-
-        for i in range(last):
-            trip(i, range(0, i + 1))
 
         def run(i, _):
             trip(i, range(last + 1))
             return 0
 
-        lax.fori_loop(last, count, run, 0)
+        for i in range(last):
+            trip(i, range(0, i + 1))
+        if hook is None:
+            lax.fori_loop(last, count, run, 0)
+        else:
+            lax.fori_loop(last, hook[0], run, 0)
+            hook[1]()
+            lax.fori_loop(hook[0], count, run, 0)
         for i in range(count, count + last):
             trip(i, range(i - count + 1, last + 1))
 
@@ -188,7 +191,8 @@
         exchange(send_p, recv_p, s2, r2, i).start()
     recv_p[mc] = send_p[mc]
 
-    heads(ST, [functools.partial(f, 1) for f in (dots, features, weigh)])
+    heads(ST, [lambda i, j: (dots(1, i, j), local(0, i, j)), functools.partial(features, 1),
+               functools.partial(weigh, 1)])
 
     arrivals(send_p, recv_p, s2, r2).wait_recv()
     for i in range(SEQS * kvl):
@@ -200,69 +204,94 @@
 
     ssq[...] = jnp.zeros_like(ssq)
 
-    def partner(s, i):
-        return lax.rem(mz + i, nz)
-
-    def scatter(s, i):
-        to = lax.rem(mz + i, nz)
+    up, far, down = (lax.rem(mz + i, nz) for i in (1, 2, 3))
+
+    def hop(s, m):
         return pltpu.make_async_remote_copy(
-            src_ref=msg.at[s, i - 1], dst_ref=got.at[s, i - 1], send_sem=s3.at[s, i], recv_sem=r3.at[s, i],
-            device_id=(mc, to), device_id_type=MESH)
-
-    def gather(s, i, at):
-        to = lax.rem(mz + i, nz)
+            src_ref=msg.at[s, m], dst_ref=got.at[s, m], send_sem=s3.at[s, m], recv_sem=r3.at[s, m],
+            device_id=(mc, up if m % 2 == 0 else down), device_id_type=MESH)
+
+    def spread(s, m, owner, half):
         return pltpu.make_async_remote_copy(
-            src_ref=red.at[s, at], dst_ref=red.at[s, at], send_sem=s4.at[s, i], recv_sem=r4.at[s, i],
-            device_id=(mc, to), device_id_type=MESH)
-
-    def project(s):
-        for i in (2, 1, 3, 0) if nz == 4 else range(nz - 1, -1, -1):
+            src_ref=red.at[s, owner, half], dst_ref=red.at[s, owner, half], send_sem=s4.at[s, m],
+            recv_sem=r4.at[s, m], device_id=(mc, up if m % 2 == 0 else down), device_id_type=MESH)
+
+    leaving = ((mz, 0), (mz, 1), (mz, 1), (mz, 0), (down, 0), (up, 1))
+    coming = ((down, 0), (up, 1), (down, 1), (up, 0), (far, 0), (far, 1))
+
+    def send(s, m, value):
+        msg[s, m] = value.astype(bf16)
+        hop(s, m).start()
+
+    def project(s, between=None):
+        for i in (2, 1, 3, 0):
             to = lax.rem(mz + i, nz)
             block = nn(rit[pl.ds(pl.multiple_of(to * rb, rb), rb), :], att[s])
-            if i == 0:
+            block = jnp.concatenate([block, ssq[s]], axis=0)
+            low, high = block[:, 0:HD], block[:, HD:]
+            if i == 2:
+                send(s, 0, low)
+                send(s, 1, high)
+                if between is not None:
+                    between()
+            elif i == 1:
+                send(s, 2, high)
+                near[s, 0] = low
+            elif i == 3:
+                send(s, 3, low)
+                near[s, 1] = high
+            else:
                 part[s] = block
-            else:
-                msg[s, i - 1, 0:rb, :] = block.astype(bf16)
-                msg[s, i - 1, rb:, :] = ssq[s].astype(bf16)
-                scatter(s, i).start()
+
+    def relay(s):
+        for m in range(2):
+            hop(s, m).wait_recv()
+            send(s, 4 + m, near[s, m] + got[s, m].astype(f32))
 
     def reduce(s):
-        for i in range(1, nz):
-            scatter(s, i).wait_recv()
-        total = part[s]
-        squares = ssq[s]
-        for i in range(1, nz):
-            total = total + got[s, i - 1, 0:rb, :].astype(f32)
-            squares = squares + got[s, i - 1, rb:, :].astype(f32)
-        factor = lax.rsqrt(jnp.sum(squares, axis=0, keepdims=True) / feats + 1e-05)
-        red[s, mz] = (total * factor).astype(bf16)
-        for i in range(1, nz):
-            gather(s, i, mz).start()
+        for half, ms in enumerate(((3, 4), (2, 5))):
+            total = part[s, :, half * HD:(half + 1) * HD]
+            for m in ms:
+                hop(s, m).wait_recv()
+                total = total + got[s, m].astype(f32)
+            factor = lax.rsqrt(jnp.sum(total[rb:], axis=0, keepdims=True) / feats + 1e-05)
+            red[s, mz, half] = (total[0:rb] * factor).astype(bf16)
+            spread(s, half, *leaving[half]).start()
+        for m in (2, 3):
+            spread(s, m, *leaving[m]).start()
+
+    def forward(s):
+        for m in range(2):
+            spread(s, m, *coming[m]).wait_recv()
+            spread(s, 4 + m, *leaving[4 + m]).start()
 
     def expand(s):
-        for i in range(1, nz):
-            gather(s, i, lax.rem(mz + nz - i, nz)).wait_recv()
-        lhs = jnp.concatenate([red[s, p].T for p in range(nz)], axis=1)
+        for m in range(2, 6):
+            spread(s, m, *coming[m]).wait_recv()
+        lhs = jnp.concatenate([jnp.concatenate([red[s, p, half].T for p in range(nz)], axis=1)
+                               for half in range(2)], axis=0)
         tile = out_ref.shape[2] // OUT_TILES
         for n in range(OUT_TILES):
             cols = slice(n * tile, (n + 1) * tile)
             out_ref[s, :, cols] = nn(lhs, ro_v[:, cols]).astype(bf16)
 
-    heads(AT, [functools.partial(f, 0) for f in (attend, divide)])
+    heads(ST, [lambda i, j: (attend(0, i, j), local(1, i, j)), functools.partial(divide, 0)])
     project(0)
-    heads(AT, [functools.partial(f, 1) for f in (attend, divide)])
-    reduce(0)
-    project(1)
+    heads(ST, [functools.partial(f, 1) for f in (attend, divide)], hook=(2, lambda: relay(0)))
+    project(1, lambda: reduce(0))
+    relay(1)
+    forward(0)
     loads[7].wait()
+    reduce(1)
     expand(0)
-    reduce(1)
+    forward(1)
     expand(1)
     arrivals(send_e, recv_e, s1, r1).wait_send()
     arrivals(send_p, recv_p, s2, r2).wait_send()
     for s in range(SEQS):
-        for i in range(1, nz):
-            scatter(s, i).wait_send()
-            gather(s, i, mz).wait_send()
+        for m in range(6):
+            hop(s, m).wait_send()
+            spread(s, m, *leaving[m]).wait_send()
 
 
 def attention(nc, nz, q, k, v, qm, km, gain, ri, ro):
@@ -270,7 +299,7 @@
     rows = SEQS * kvl * HD // nc
     rb = rank // nz
     states = SEQS * kvl
-    st, at = min(ST, hl), min(AT, hl)
+    st = min(ST, hl)
     vm, dma = pltpu.VMEM, pltpu.SemaphoreType.DMA
     hbm = pl.BlockSpec(memory_space=pltpu.HBM)
     vmem = pl.BlockSpec(memory_space=pltpu.VMEM)
@@ -284,17 +313,16 @@
             vm(km.shape, bf16), vm(ri.shape, bf16), vm(ro.shape, bf16),
             vm((rank, hl * HD), bf16), vm((hl, HD, HD), f32), vm((hl, HD), f32),
             vm((states, BLK, 2 * HD), bf16), vm((states, HD + 16, BLK), bf16), vm((states, HD + 16, 2 * HD), bf16),
-            vm((SEQS, hl * HD, BLK), bf16), vm((SEQS, 16, BLK), f32), vm((SEQS, rb, BLK), f32),
+            vm((SEQS, hl * HD, BLK), bf16), vm((SEQS, 16, BLK), f32), vm((SEQS, rb + 16, BLK), f32),
             vm((nc, rows, 3 * HD), bf16), vm((nc, rows, 3 * HD), bf16),
             vm((nc, rows, 3 * HD), bf16), vm((nc, rows, 3 * HD), bf16),
-            vm((SEQS, nz - 1, rb + 16, BLK), bf16), vm((SEQS, nz - 1, rb + 16, BLK), bf16),
-            vm((SEQS, nz, rb, BLK), bf16), vm((HD, HD), bf16),
-            vm((st, HD, BLK), f32), vm((at, HD + 16, BLK), f32),
+            vm((SEQS, 6, rb + 16, HD), bf16), vm((SEQS, 6, rb + 16, HD), bf16),
+            vm((SEQS, nz, 2, rb, HD), bf16), vm((HD, HD), bf16),
+            vm((st, HD, BLK), f32), vm((st, HD + 16, BLK), f32), vm((SEQS, 2, rb + 16, HD), f32),
             dma((8,)), dma, dma, dma, dma,
-            dma((SEQS, nz)), dma((SEQS, nz)), dma((SEQS, nz)), dma((SEQS, nz)),
+            dma((SEQS, 6)), dma((SEQS, 6)), dma((SEQS, 6)), dma((SEQS, 6)),
         ] + [vm((SEQS * hl // st, 2, 2 * HD, HD), bf16)] * st + [
-            vm((SEQS * hl // st, 2, BLK, HD), bf16)] * st + [
-        ],
+            vm((SEQS * hl // st, 2, BLK, HD), bf16)] * st + [vm((hl // st, HD + 16, BLK), f32)] * st,
         compiler_params=pltpu.CompilerParams(
             collective_id=0, has_side_effects=True, vmem_limit_bytes=VLIM * 2**20),
         name="attention",

time: 50.1 us -> 50.5 us (level)
  no operation moved by 1% of the time
where the time goes in v4:
time: 50.5 us; the launch traced here: 50.3 us
  Pallas kernels  48.3 us (96%)
  local copies, waits for them, and re-layouts  2.02 us (4%)
    pallas_call x1, Pallas kernels, attention(): pl.pallas_call(functools.partial(kernel, nc, nz, float(nz * hl * HD)), ou...  48.3 us
    unnamed x1, local copies, waits for them, and re-layouts  2.02 us

profile of v4, /device:TPU:0, one launch (start us, length us, event | category | flops | bytes accessed | tf_op | source)
XLA Modules:
  0.0 50.3 jit_solution(1917540157741675640)
XLA Ops:
  0.0 48.3 %attention.1 = bf16[2,256,4096]{2,1,0:T(8,128)(2,1)S(1)} custom-call(bf16[2,256,4096]{2,1,0:T(8,128)(2,1)} %q_hbm.1, bf16[2,256,256]{2,1,0:T(8,128)(2,1)} %k_hbm.1, bf16[2,256,256]{2,1,0:T(8,128)(2,1)} %v_hbm.1, bf16[32,128,128]{2,1,0:T(8,128)(2,1)} %qm_hbm.1, bf16[2,128,128]{2,1,0:T(8,128)(2,1)} %km_hbm.1, bf16[32,128]{1,0:T(8,128)(2,1)} %bitcast.1, ...), custom_call_target="tpu_custom_call" | custom-call | tf_op jit(solution)/shard_map/attention/pallas_call | solution.py:306
  48.3 2.0 %copy.10 = bf16[2,256,4096]{2,1,0:T(8,128)(2,1)} copy(bf16[2,256,4096]{2,1,0:T(8,128)(2,1)S(1)} %attention.1) | data formatting | bytes 8388608

commit v5 on v4

--- a/solution.py
+++ b/solution.py
@@ -35,7 +35,7 @@
 def kernel(nc, nz, feats, q_hbm, k_hbm, v_hbm, qm_hbm, km_hbm, gain_ref, ri_hbm, ro_hbm, out_ref,
            q_v, k_v, v_v, qm_v, km_v, ri_v, ro_v, rit, gcol, gains, fk, vta, pta, att, ssq, part,
            send_e, recv_e, send_p, recv_p, msg, got, red,
-           tri, raw, tot, near, in_sem, s1, r1, s2, r2, s3, r3, s4, r4, *per_head):
+           tri, raw, tot, in_sem, s1, r1, s2, r2, s3, r3, s4, r4, *per_head):
     n = len(per_head) // 3
     fq, wb, loc = per_head[:n], per_head[n:2 * n], per_head[2 * n:]
     hl, kvl = qm_v.shape[0], km_v.shape[0]
@@ -143,13 +143,19 @@
     def attend(s, i, j):
         tot[j] = loc[j][i] + nn(pta[s * kvl + (i * ST + j) // groups], joined(fq[j], s * (hl // ST) + i))
 
-    def divide(s, i, j):
+    def attend_half(s, c, i, j):
+        lanes = slice(c * HD, (c + 1) * HD)
+        tot[j, :, lanes] = loc[j][i, :, lanes] + nn(
+            pta[s * kvl + (i * ST + j) // groups], fq[j][s * (hl // ST) + i, c])
+
+    def divide(s, cs, i, j):
         h = i * ST + j
-        out = tot[j, 0:HD] * (1.0 / tot[j, HD:HD + 1])
-        ssq[s] += jnp.sum((out * out).reshape(HD // 16, 16, BLK), axis=0)
         scale = gcol[h]
-        att[s, lanes_of(h), :] = jnp.concatenate(
-            [out[:, 0:HD] * scale, out[:, HD:] * scale], axis=1).astype(bf16)
+        for c in cs:
+            lanes = slice(c * HD, (c + 1) * HD)
+            out = tot[j, 0:HD, lanes] * (1.0 / tot[j, HD:HD + 1, lanes])
+            ssq[s, :, lanes] += jnp.sum((out * out).reshape(HD // 16, 16, HD), axis=0)
+            att[s, c, lanes_of(h), :] = (out * scale).astype(bf16)
 
     def heads(step, stages, hook=None):
         last, count = len(stages) - 1, hl // step
@@ -204,94 +210,75 @@
 
     ssq[...] = jnp.zeros_like(ssq)
 
-    up, far, down = (lax.rem(mz + i, nz) for i in (1, 2, 3))
-
-    def hop(s, m):
+    def scatter(s, c, i):
+        to = lax.rem(mz + i, nz)
         return pltpu.make_async_remote_copy(
-            src_ref=msg.at[s, m], dst_ref=got.at[s, m], send_sem=s3.at[s, m], recv_sem=r3.at[s, m],
-            device_id=(mc, up if m % 2 == 0 else down), device_id_type=MESH)
-
-    def spread(s, m, owner, half):
+            src_ref=msg.at[s, c, i - 1], dst_ref=got.at[s, c, i - 1], send_sem=s3.at[2 * s + c, i],
+            recv_sem=r3.at[2 * s + c, i], device_id=(mc, to), device_id_type=MESH)
+
+    def gather(s, c, i, at):
+        to = lax.rem(mz + i, nz)
         return pltpu.make_async_remote_copy(
-            src_ref=red.at[s, owner, half], dst_ref=red.at[s, owner, half], send_sem=s4.at[s, m],
-            recv_sem=r4.at[s, m], device_id=(mc, up if m % 2 == 0 else down), device_id_type=MESH)
-
-    leaving = ((mz, 0), (mz, 1), (mz, 1), (mz, 0), (down, 0), (up, 1))
-    coming = ((down, 0), (up, 1), (down, 1), (up, 0), (far, 0), (far, 1))
-
-    def send(s, m, value):
-        msg[s, m] = value.astype(bf16)
-        hop(s, m).start()
-
-    def project(s, between=None):
-        for i in (2, 1, 3, 0):
+            src_ref=red.at[s, at, c], dst_ref=red.at[s, at, c], send_sem=s4.at[2 * s + c, i],
+            recv_sem=r4.at[2 * s + c, i], device_id=(mc, to), device_id_type=MESH)
+
+    order = (2, 1, 3)
+    half = (slice(0, HD), slice(HD, BLK))
+
+    def project(s, cs):
+        rhs = jnp.concatenate([att[s, c] for c in cs], axis=1)
+        for i in order + (0,):
             to = lax.rem(mz + i, nz)
-            block = nn(rit[pl.ds(pl.multiple_of(to * rb, rb), rb), :], att[s])
-            block = jnp.concatenate([block, ssq[s]], axis=0)
-            low, high = block[:, 0:HD], block[:, HD:]
-            if i == 2:
-                send(s, 0, low)
-                send(s, 1, high)
-                if between is not None:
-                    between()
-            elif i == 1:
-                send(s, 2, high)
-                near[s, 0] = low
-            elif i == 3:
-                send(s, 3, low)
-                near[s, 1] = high
-            else:
-                part[s] = block
-
-    def relay(s):
-        for m in range(2):
-            hop(s, m).wait_recv()
-            send(s, 4 + m, near[s, m] + got[s, m].astype(f32))
-
-    def reduce(s):
-        for half, ms in enumerate(((3, 4), (2, 5))):
-            total = part[s, :, half * HD:(half + 1) * HD]
-            for m in ms:
-                hop(s, m).wait_recv()
-                total = total + got[s, m].astype(f32)
-            factor = lax.rsqrt(jnp.sum(total[rb:], axis=0, keepdims=True) / feats + 1e-05)
-            red[s, mz, half] = (total[0:rb] * factor).astype(bf16)
-            spread(s, half, *leaving[half]).start()
-        for m in (2, 3):
-            spread(s, m, *leaving[m]).start()
-
-    def forward(s):
-        for m in range(2):
-            spread(s, m, *coming[m]).wait_recv()
-            spread(s, 4 + m, *leaving[4 + m]).start()
-
-    def expand(s):
-        for m in range(2, 6):
-            spread(s, m, *coming[m]).wait_recv()
-        lhs = jnp.concatenate([jnp.concatenate([red[s, p, half].T for p in range(nz)], axis=1)
-                               for half in range(2)], axis=0)
+            block = nn(rit[pl.ds(pl.multiple_of(to * rb, rb), rb), :], rhs)
+            for n, c in enumerate(cs):
+                piece = jnp.concatenate([block[:, n * HD:(n + 1) * HD], ssq[s, :, half[c]]], axis=0)
+                if i == 0:
+                    part[s, :, half[c]] = piece
+                else:
+                    msg[s, c, i - 1] = piece.astype(bf16)
+                    scatter(s, c, i).start()
+
+    def reduce(s, c):
+        total = part[s, :, half[c]]
+        for i in order:
+            scatter(s, c, i).wait_recv()
+            total = total + got[s, c, i - 1].astype(f32)
+        factor = lax.rsqrt(jnp.sum(total[rb:], axis=0, keepdims=True) / feats + 1e-05)
+        red[s, mz, c] = (total[0:rb] * factor).astype(bf16)
+        for i in order:
+            gather(s, c, i, mz).start()
+
+    def expand(s, cs):
+        for c in cs:
+            for i in order:
+                gather(s, c, i, lax.rem(mz + nz - i, nz)).wait_recv()
+        lhs = jnp.concatenate([jnp.concatenate([red[s, p, c].T for p in range(nz)], axis=1) for c in cs], axis=0)
         tile = out_ref.shape[2] // OUT_TILES
         for n in range(OUT_TILES):
             cols = slice(n * tile, (n + 1) * tile)
-            out_ref[s, :, cols] = nn(lhs, ro_v[:, cols]).astype(bf16)
-
-    heads(ST, [lambda i, j: (attend(0, i, j), local(1, i, j)), functools.partial(divide, 0)])
-    project(0)
-    heads(ST, [functools.partial(f, 1) for f in (attend, divide)], hook=(2, lambda: relay(0)))
-    project(1, lambda: reduce(0))
-    relay(1)
-    forward(0)
+            out_ref[s, cs[0] * HD:(cs[-1] + 1) * HD, cols] = nn(lhs, ro_v[:, cols]).astype(bf16)
+
+    both = (0, 1)
+    heads(ST, [lambda i, j: (attend(0, i, j), local(1, i, j)), functools.partial(divide, 0, both)])
+    project(0, both)
+    heads(ST, [functools.partial(attend_half, 1, 0), functools.partial(divide, 1, (0,))])
+    project(1, (0,))
+    heads(ST, [functools.partial(attend_half, 1, 1), functools.partial(divide, 1, (1,))],
+          hook=(2, lambda: (reduce(0, 0), reduce(0, 1))))
+    project(1, (1,))
     loads[7].wait()
-    reduce(1)
-    expand(0)
-    forward(1)
-    expand(1)
+    reduce(1, 0)
+    expand(0, both)
+    reduce(1, 1)
+    expand(1, (0,))
+    expand(1, (1,))
     arrivals(send_e, recv_e, s1, r1).wait_send()
     arrivals(send_p, recv_p, s2, r2).wait_send()
     for s in range(SEQS):
-        for m in range(6):
-            hop(s, m).wait_send()
-            spread(s, m, *leaving[m]).wait_send()
+        for c in both:
+            for i in order:
+                scatter(s, c, i).wait_send()
+                gather(s, c, i, mz).wait_send()
 
 
 def attention(nc, nz, q, k, v, qm, km, gain, ri, ro):
@@ -313,14 +300,14 @@
             vm(km.shape, bf16), vm(ri.shape, bf16), vm(ro.shape, bf16),
             vm((rank, hl * HD), bf16), vm((hl, HD, HD), f32), vm((hl, HD), f32),
             vm((states, BLK, 2 * HD), bf16), vm((states, HD + 16, BLK), bf16), vm((states, HD + 16, 2 * HD), bf16),
-            vm((SEQS, hl * HD, BLK), bf16), vm((SEQS, 16, BLK), f32), vm((SEQS, rb + 16, BLK), f32),
+            vm((SEQS, 2, hl * HD, HD), bf16), vm((SEQS, 16, BLK), f32), vm((SEQS, rb + 16, BLK), f32),
             vm((nc, rows, 3 * HD), bf16), vm((nc, rows, 3 * HD), bf16),
             vm((nc, rows, 3 * HD), bf16), vm((nc, rows, 3 * HD), bf16),
-            vm((SEQS, 6, rb + 16, HD), bf16), vm((SEQS, 6, rb + 16, HD), bf16),
+            vm((SEQS, 2, nz - 1, rb + 16, HD), bf16), vm((SEQS, 2, nz - 1, rb + 16, HD), bf16),
             vm((SEQS, nz, 2, rb, HD), bf16), vm((HD, HD), bf16),
-            vm((st, HD, BLK), f32), vm((st, HD + 16, BLK), f32), vm((SEQS, 2, rb + 16, HD), f32),
+            vm((st, HD, BLK), f32), vm((st, HD + 16, BLK), f32),
             dma((8,)), dma, dma, dma, dma,
-            dma((SEQS, 6)), dma((SEQS, 6)), dma((SEQS, 6)), dma((SEQS, 6)),
+            dma((2 * SEQS, nz)), dma((2 * SEQS, nz)), dma((2 * SEQS, nz)), dma((2 * SEQS, nz)),
         ] + [vm((SEQS * hl // st, 2, 2 * HD, HD), bf16)] * st + [
             vm((SEQS * hl // st, 2, BLK, HD), bf16)] * st + [vm((hl // st, HD + 16, BLK), f32)] * st,
         compiler_params=pltpu.CompilerParams(

time: 50.5 us -> 47.3 us (0.937)
  Pallas kernels: 48.3 us -> 45.1 us
    pallas_call x1, Pallas kernels: 48.3 us -> 45.1 us  [attention(): pl.pallas_call(functools.partial(kernel, nc, nz, float(nz * hl * HD)), ou...]
where the time goes in v5:
time: 47.3 us; the launch traced here: 47.1 us
  Pallas kernels  45.1 us (95%)
  local copies, waits for them, and re-layouts  2.02 us (4%)
    pallas_call x1, Pallas kernels, attention(): pl.pallas_call(functools.partial(kernel, nc, nz, float(nz * hl * HD)), ou...  45.1 us
    unnamed x1, local copies, waits for them, and re-layouts  2.02 us

profile of v5, /device:TPU:0, one launch (start us, length us, event | category | flops | bytes accessed | tf_op | source)
XLA Modules:
  0.0 47.1 jit_solution(829812288747937660)
XLA Ops:
  0.0 45.1 %attention.1 = bf16[2,256,4096]{2,1,0:T(8,128)(2,1)S(1)} custom-call(bf16[2,256,4096]{2,1,0:T(8,128)(2,1)} %q_hbm.1, bf16[2,256,256]{2,1,0:T(8,128)(2,1)} %k_hbm.1, bf16[2,256,256]{2,1,0:T(8,128)(2,1)} %v_hbm.1, bf16[32,128,128]{2,1,0:T(8,128)(2,1)} %qm_hbm.1, bf16[2,128,128]{2,1,0:T(8,128)(2,1)} %km_hbm.1, bf16[32,128]{1,0:T(8,128)(2,1)} %bitcast.1, ...), custom_call_target="tpu_custom_call" | custom-call | tf_op jit(solution)/shard_map/attention/pallas_call | solution.py:293
  45.1 2.0 %copy.10 = bf16[2,256,4096]{2,1,0:T(8,128)(2,1)} copy(bf16[2,256,4096]{2,1,0:T(8,128)(2,1)S(1)} %attention.1) | data formatting | bytes 8388608

commit v6 on v5

--- a/solution.py
+++ b/solution.py
@@ -35,7 +35,7 @@
 def kernel(nc, nz, feats, q_hbm, k_hbm, v_hbm, qm_hbm, km_hbm, gain_ref, ri_hbm, ro_hbm, out_ref,
            q_v, k_v, v_v, qm_v, km_v, ri_v, ro_v, rit, gcol, gains, fk, vta, pta, att, ssq, part,
            send_e, recv_e, send_p, recv_p, msg, got, red,
-           tri, raw, tot, in_sem, s1, r1, s2, r2, s3, r3, s4, r4, *per_head):
+           tri, raw, tot, send_k, recv_k, sk, rk, in_sem, s1, r1, s2, r2, s3, r3, s4, r4, *per_head):
     n = len(per_head) // 3
     fq, wb, loc = per_head[:n], per_head[n:2 * n], per_head[2 * n:]
     hl, kvl = qm_v.shape[0], km_v.shape[0]
@@ -65,7 +65,6 @@
 
     for load in loads[:3]:
         load.wait()
-    first = lax.broadcasted_iota(jnp.int32, (rows, HD), 0) == 0
     for s in range(SEQS):
         for g in range(kvl):
             i = s * kvl + g
@@ -78,9 +77,9 @@
             state = nn(vta[i], fk[i])
             for p in range(per):
                 j = i * per + p
-                send_e[j, :, 0:2 * HD] = state[p * rows:(p + 1) * rows].astype(bf16)
-                send_e[j, :, 2 * HD:] = jnp.where(
-                    first, state[HD:HD + 1, 0:HD], state[HD:HD + 1, HD:2 * HD]).astype(bf16)
+                send_e[j] = state[p * rows:(p + 1) * rows].astype(bf16)
+            send_k[2 * i:2 * i + 1, :] = state[HD:HD + 1, 0:HD]
+            send_k[2 * i + 1:2 * i + 2, :] = state[HD:HD + 1, HD:]
 
     pl.semaphore_wait(barrier, nc - 1 + nz - 1)
 
@@ -97,7 +96,13 @@
 
     for i in range(1, nc):
         exchange(send_e, recv_e, s1, r1, i).start()
+    for i in range(1, nc):
+        to = lax.rem(mc + i, nc)
+        pltpu.make_async_remote_copy(
+            src_ref=send_k, dst_ref=recv_k.at[mc], send_sem=sk, recv_sem=rk,
+            device_id=(to, mz), device_id_type=MESH).start()
     recv_e[mc] = send_e[mc]
+    recv_k[mc] = send_k[...]
 
     for load in loads[3:6]:
         load.wait()
@@ -200,13 +205,14 @@
     heads(ST, [lambda i, j: (dots(1, i, j), local(0, i, j)), functools.partial(features, 1),
                functools.partial(weigh, 1)])
 
+    arrivals(recv_k, recv_k, sk, rk).wait_recv()
+    sums = lax.fori_loop(0, mc, lambda i, total: total + recv_k[i], jnp.zeros(send_k.shape, f32))
     arrivals(send_p, recv_p, s2, r2).wait_recv()
     for i in range(SEQS * kvl):
         for p in range(per):
-            pta[i, p * rows:(p + 1) * rows, :] = recv_p[i * per + p, :, 0:2 * HD]
-        sums = recv_p[i * per, 0:2, 2 * HD:].astype(f32)
+            pta[i, p * rows:(p + 1) * rows, :] = recv_p[i * per + p]
         pta[i, HD:HD + 16, :] = jnp.broadcast_to(
-            jnp.concatenate([sums[0:1], sums[1:2]], axis=1), (16, BLK)).astype(bf16)
+            jnp.concatenate([sums[2 * i:2 * i + 1], sums[2 * i + 1:2 * i + 2]], axis=1), (16, BLK)).astype(bf16)
 
     ssq[...] = jnp.zeros_like(ssq)
 
@@ -274,6 +280,7 @@
     expand(1, (1,))
     arrivals(send_e, recv_e, s1, r1).wait_send()
     arrivals(send_p, recv_p, s2, r2).wait_send()
+    arrivals(recv_k, recv_k, sk, rk).wait_send()
     for s in range(SEQS):
         for c in both:
             for i in order:
@@ -301,11 +308,12 @@
             vm((rank, hl * HD), bf16), vm((hl, HD, HD), f32), vm((hl, HD), f32),
             vm((states, BLK, 2 * HD), bf16), vm((states, HD + 16, BLK), bf16), vm((states, HD + 16, 2 * HD), bf16),
             vm((SEQS, 2, hl * HD, HD), bf16), vm((SEQS, 16, BLK), f32), vm((SEQS, rb + 16, BLK), f32),
-            vm((nc, rows, 3 * HD), bf16), vm((nc, rows, 3 * HD), bf16),
-            vm((nc, rows, 3 * HD), bf16), vm((nc, rows, 3 * HD), bf16),
+            vm((nc, rows, 2 * HD), bf16), vm((nc, rows, 2 * HD), bf16),
+            vm((nc, rows, 2 * HD), bf16), vm((nc, rows, 2 * HD), bf16),
             vm((SEQS, 2, nz - 1, rb + 16, HD), bf16), vm((SEQS, 2, nz - 1, rb + 16, HD), bf16),
             vm((SEQS, nz, 2, rb, HD), bf16), vm((HD, HD), bf16),
             vm((st, HD, BLK), f32), vm((st, HD + 16, BLK), f32),
+            vm((2 * states, HD), f32), vm((nc, 2 * states, HD), f32), dma, dma,
             dma((8,)), dma, dma, dma, dma,
             dma((2 * SEQS, nz)), dma((2 * SEQS, nz)), dma((2 * SEQS, nz)), dma((2 * SEQS, nz)),
         ] + [vm((SEQS * hl // st, 2, 2 * HD, HD), bf16)] * st + [

time: 47.3 us -> 45.4 us (0.960)
  Pallas kernels: 45.1 us -> 43.2 us
    pallas_call x1, Pallas kernels: 45.1 us -> 43.2 us  [attention(): pl.pallas_call(functools.partial(kernel, nc, nz, float(nz * hl * HD)), ou...]
where the time goes in v6:
time: 45.4 us; the launch traced here: 45.2 us
  Pallas kernels  43.2 us (95%)
  local copies, waits for them, and re-layouts  2.02 us (4%)
    pallas_call x1, Pallas kernels, attention(): pl.pallas_call(functools.partial(kernel, nc, nz, float(nz * hl * HD)), ou...  43.2 us
    unnamed x1, local copies, waits for them, and re-layouts  2.02 us

profile of v6, /device:TPU:0, one launch (start us, length us, event | category | flops | bytes accessed | tf_op | source)
XLA Modules:
  0.0 45.2 jit_solution(360088599334906302)
XLA Ops:
  0.0 43.2 %attention.1 = bf16[2,256,4096]{2,1,0:T(8,128)(2,1)S(1)} custom-call(bf16[2,256,4096]{2,1,0:T(8,128)(2,1)} %q_hbm.1, bf16[2,256,256]{2,1,0:T(8,128)(2,1)} %k_hbm.1, bf16[2,256,256]{2,1,0:T(8,128)(2,1)} %v_hbm.1, bf16[32,128,128]{2,1,0:T(8,128)(2,1)} %qm_hbm.1, bf16[2,128,128]{2,1,0:T(8,128)(2,1)} %km_hbm.1, bf16[32,128]{1,0:T(8,128)(2,1)} %bitcast.1, ...), custom_call_target="tpu_custom_call" | custom-call | tf_op jit(solution)/shard_map/attention/pallas_call | solution.py:300
  43.2 2.0 %copy.10 = bf16[2,256,4096]{2,1,0:T(8,128)(2,1)} copy(bf16[2,256,4096]{2,1,0:T(8,128)(2,1)S(1)} %attention.1) | data formatting | bytes 8388608

commit v7 on v6

--- a/solution.py
+++ b/solution.py
@@ -65,6 +65,7 @@
 
     for load in loads[:3]:
         load.wait()
+    sums = []
     for s in range(SEQS):
         for g in range(kvl):
             i = s * kvl + g
@@ -78,8 +79,8 @@
             for p in range(per):
                 j = i * per + p
                 send_e[j] = state[p * rows:(p + 1) * rows].astype(bf16)
-            send_k[2 * i:2 * i + 1, :] = state[HD:HD + 1, 0:HD]
-            send_k[2 * i + 1:2 * i + 2, :] = state[HD:HD + 1, HD:]
+            sums += [state[HD:HD + 1, 0:HD], state[HD:HD + 1, HD:]]
+    send_k[...] = jnp.concatenate(sums, axis=0).astype(bf16)
 
     pl.semaphore_wait(barrier, nc - 1 + nz - 1)
 
@@ -206,7 +207,7 @@
                functools.partial(weigh, 1)])
 
     arrivals(recv_k, recv_k, sk, rk).wait_recv()
-    sums = lax.fori_loop(0, mc, lambda i, total: total + recv_k[i], jnp.zeros(send_k.shape, f32))
+    sums = lax.fori_loop(0, mc, lambda i, total: total + recv_k[i].astype(f32), jnp.zeros(send_k.shape, f32))
     arrivals(send_p, recv_p, s2, r2).wait_recv()
     for i in range(SEQS * kvl):
         for p in range(per):
@@ -313,7 +314,7 @@
             vm((SEQS, 2, nz - 1, rb + 16, HD), bf16), vm((SEQS, 2, nz - 1, rb + 16, HD), bf16),
             vm((SEQS, nz, 2, rb, HD), bf16), vm((HD, HD), bf16),
             vm((st, HD, BLK), f32), vm((st, HD + 16, BLK), f32),
-            vm((2 * states, HD), f32), vm((nc, 2 * states, HD), f32), dma, dma,
+            vm((2 * states, HD), bf16), vm((nc, 2 * states, HD), bf16), dma, dma,
             dma((8,)), dma, dma, dma, dma,
             dma((2 * SEQS, nz)), dma((2 * SEQS, nz)), dma((2 * SEQS, nz)), dma((2 * SEQS, nz)),
         ] + [vm((SEQS * hl // st, 2, 2 * HD, HD), bf16)] * st + [

time: 45.4 us -> 45.2 us (level)
  no operation moved by 1% of the time
where the time goes in v7:
time: 45.2 us; the launch traced here: 45 us
  Pallas kernels  43 us (95%)
  local copies, waits for them, and re-layouts  2.02 us (4%)
    pallas_call x1, Pallas kernels, attention(): pl.pallas_call(functools.partial(kernel, nc, nz, float(nz * hl * HD)), ou...  43 us
    unnamed x1, local copies, waits for them, and re-layouts  2.02 us

profile of v7, /device:TPU:0, one launch (start us, length us, event | category | flops | bytes accessed | tf_op | source)
XLA Modules:
  0.0 45.0 jit_solution(12738689363689017609)
XLA Ops:
  0.0 43.0 %attention.1 = bf16[2,256,4096]{2,1,0:T(8,128)(2,1)S(1)} custom-call(bf16[2,256,4096]{2,1,0:T(8,128)(2,1)} %q_hbm.1, bf16[2,256,256]{2,1,0:T(8,128)(2,1)} %k_hbm.1, bf16[2,256,256]{2,1,0:T(8,128)(2,1)} %v_hbm.1, bf16[32,128,128]{2,1,0:T(8,128)(2,1)} %qm_hbm.1, bf16[2,128,128]{2,1,0:T(8,128)(2,1)} %km_hbm.1, bf16[32,128]{1,0:T(8,128)(2,1)} %bitcast.1, ...), custom_call_target="tpu_custom_call" | custom-call | tf_op jit(solution)/shard_map/attention/pallas_call | solution.py:301
  43.0 2.0 %copy.10 = bf16[2,256,4096]{2,1,0:T(8,128)(2,1)} copy(bf16[2,256,4096]{2,1,0:T(8,128)(2,1)S(1)} %attention.1) | data formatting | bytes 8388608
